TPU v7x, 512 devices: a whole 4x4x16 slice. The times are simulated.
512 devices in a mesh: occ: 64 (over z_lo, y, core), aux: 8 (over x, z_hi).
Axes of the slice: x: 4, y: 4, z: 16 (z_hi: 2, z_lo: 8; z = z_hi * 8 + z_lo), core: 2. Of those that a mesh axis runs over, the one named last changes fastest.
Arguments:
- half_blocks: bfloat16 [1536, 64, 6144], P('occ', None, 'aux'), may hold values from -0.796875 to 0.796875
- block_rows: int32 [64], replicated, may hold values from 1 to 24, 768 in all
- block_order: int32 [64], replicated, may hold values from 0 to 63, each once
- ao_to_virt: bfloat16 [768, 512], replicated, may hold values from -0.21875 to 0.21875
- occ_energy: float32 [64], replicated, may hold values from -2 to -0.5
- virt_energy: float32 [512], replicated, may hold values from 0.2 to 3
Outputs:
- gamma: float32 [64, 512, 6144], P('occ', None, 'aux')
Inputs may be any that keep to these rules, and one draw needn't show every extreme that they name: block_rows[s] is the number of AO functions held by device s of occ; the counts sum to 768 and one of them equals 24. A permutation; the runs of AO functions lie end to end in the order of block_order.
All inputs are finite; a program needn't handle non-finite values.
Results may differ from a plain program's by a relative error of at most 0.008.
Values may be sent and summed in bfloat16 or wider, within the bound.
No kernel may reach another device: no remote copies, remote signals or barrier semaphores. Data moves between devices by JAX's collectives and lax.ppermute only.
A program may use at most 64 MiB of HBM per device.

v0:
```python
import jax
import jax.numpy as jnp
from jax import lax
from jax.sharding import PartitionSpec as P

CYCLE = 3


def shifted(value, axis, by):
    devices = lax.axis_size(axis)
    return lax.ppermute(value, axis, [(i, (i + by) % devices) for i in range(devices)])


def ao_layout(block_rows, block_order, maxrows):
    device_count = block_rows.shape[0]
    matches = block_order[:, None] == jnp.arange(device_count, dtype=jnp.int32)[None, :]
    ordered = jnp.sum(jnp.where(matches, block_rows[None, :], 0), axis=1)
    before = jnp.cumsum(ordered) - ordered
    starts = jnp.sum(jnp.where(matches, before[:, None], 0), axis=0)
    offset = jnp.arange(maxrows, dtype=jnp.int32)
    in_block = offset[None, :] < block_rows[:, None]
    target = starts[:, None] + offset[None, :]
    return (in_block, target)


def build_table(block_rows, block_order, ao_to_virt, maxrows):
    in_block, target = ao_layout(block_rows, block_order, maxrows)
    row_index = jnp.where(in_block, target, 0).reshape(-1)
    ao_rows = jnp.take(ao_to_virt, row_index, axis=0)
    return jnp.where(in_block.reshape(-1, 1), ao_rows, jnp.zeros_like(ao_rows))


def contract_rows(ao_table, received):
    return lax.dot_general(
        ao_table, received, (((0,), (0,)), ((), ())), preferred_element_type=jnp.float32
    ).astype(jnp.bfloat16)


def shards(half_blocks, block_rows, block_order, ao_to_virt, occ_energy, virt_energy):
    maxrows = half_blocks.shape[0]
    device_count = occ_energy.shape[0]
    position = lax.axis_index("occ")
    ao_table = build_table(block_rows, block_order, ao_to_virt, maxrows)
    own_tile = contract_rows(
        ao_table,
        lax.all_to_all(half_blocks, "occ", split_axis=1, concat_axis=0, tiled=True)[:, 0, :],
    )
    density = jnp.zeros(own_tile.shape, jnp.float32)
    other_tile = own_tile
    for cycle_step in range(CYCLE + 1):
        if cycle_step > 0:
            other_tile = shifted(other_tile, "occ", 1)
        partner = (position - cycle_step) % device_count
        energy_gap = (
            virt_energy[:, None] + virt_energy[None, :] - occ_energy[position] - occ_energy[partner]
        )
        product = lax.dot_general(
            own_tile, other_tile, (((1,), (1,)), ((), ())), preferred_element_type=jnp.float32
        )
        partial_value = 2.0 * product - product.T
        merged = lax.psum(partial_value.astype(jnp.bfloat16), "aux").astype(jnp.float32)
        amplitudes = (merged / energy_gap).astype(jnp.bfloat16)
        density = density + jnp.dot(amplitudes, other_tile, preferred_element_type=jnp.float32)
    return density[None]


def solution(mesh):
    return jax.shard_map(
        shards,
        mesh=mesh,
        in_specs=(P("occ", None, "aux"), P(), P(), P(), P(), P()),
        out_specs=P("occ", None, "aux"),
        check_vma=False,
    )
```

profile of v0, /device:TPU:1, one launch (start us, length us, event | category | flops | bytes accessed | tf_op | source)
XLA Modules:
  0.0 594.4 jit_solution(5116064361449036951)
XLA Ops:
  6.5 4.4 copy.19
  11.0 17.5 %all-to-all-start = ((bf16[24,64,768]{2,0,1:T(8,128)(2,1)}), bf16[24,64,768]{2,0,1:T(8,128)(2,1)}, u32[]{:S(2)}, u32[]{:S(2)}) async-start(bf16[24,64,768]{2,0,1:T(8,128)(2,1)} %copy.19), calls=%async_computation | async-start | bytes 4718592 | tf_op jit(solution)/shard_map/all_to_all | solution.py:46
  28.6 0.2 select_reduce_fusion.1
  28.9 0.1 reduce
  29.7 4.8 gather_fusion
  34.5 100.6 %all-to-all-done = bf16[24,64,768]{2,0,1:T(8,128)(2,1)} async-done(((bf16[24,64,768]{2,0,1:T(8,128)(2,1)}), bf16[24,64,768]{2,0,1:T(8,128)(2,1)}, u32[]{:S(2)}, u32[]{:S(2)}) %all-to-all-start) | async-done | bytes 2359328 | tf_op jit(solution)/shard_map/all_to_all | solution.py:46
  135.1 3.4 fusion.5
  138.5 4.3 collective-permute-start
  142.8 8.9 %collective-permute-done = bf16[512,768]{1,0:T(8,128)(2,1)S(1)} collective-permute-done((bf16[512,768]{1,0:T(8,128)(2,1)S(1)}, bf16[512,768]{1,0:T(8,128)(2,1)S(1)}, u32[]{:S(2)}, u32[]{:S(2)}) %collective-permute-start) | collective-permute-done | bytes 786464 | tf_op jit(solution)/shard_map/ppermute | solution.py:11
  151.7 4.4 collective-permute-start.1
  156.1 0.6 fusion.37
  156.7 1.3 copy.20
  158.0 2.3 fusion.11
  160.3 0.6 fusion.38
  160.9 1.3 copy.21
  162.2 3.4 collective-permute-done.1
  165.6 4.0 collective-permute-start.2
  169.6 2.3 fusion.10
  171.9 1.7 fusion.39
  173.7 1.3 copy.22
  175.0 2.3 fusion.9
  177.2 10.5 %collective-permute-done.2 = bf16[512,768]{1,0:T(8,128)(2,1)S(1)} collective-permute-done((bf16[512,768]{1,0:T(8,128)(2,1)}, bf16[512,768]{1,0:T(8,128)(2,1)S(1)}, u32[]{:S(2)}, u32[]{:S(2)}) %collective-permute-start.2) | collective-permute-done | bytes 786464 | tf_op jit(solution)/shard_map/ppermute | solution.py:11
  187.8 0.6 fusion.40
  188.4 1.3 copy.23
  189.7 2.3 fusion.8
  192.1 0.6 copy-done.4
  192.6 0.7 fusion.36
  193.3 382.2 %all-reduce.3.cloned.1.call-done = (bf16[512,512]{0,1:T(8,128)(2,1)}, bf16[512,512]{0,1:T(8,128)(2,1)}, bf16[512,512]{0,1:T(8,128)(2,1)}, bf16[512,512]{0,1:T(8,128)(2,1)}) async-done(((bf16[512,512]{0,1:T(8,128)(2,1)}, bf16[512,512]{0,1:T(8,128)(2,1)}, bf16[512,512]{0,1:T(8,128)(2,1)}, bf16[512,512]{0,1:T(8,128)(2,1)}), (bf16[512,512]{0,1:T(8,128)(2,1)}, bf16[512,512]{0,1:T(8,128)(2,1)}, ...) | async-done | bytes 2097168 | tf_op jit(solution)/shard_map/psum | solution.py:61
  575.5 3.3 fusion.14
  578.8 2.2 fusion.15
  581.0 3.2 fusion.16
  584.2 3.3 add_bitcast_fusion
  (33 shorter events, 0.9 us)
Async XLA Ops:
  6.5 23.1 %copy-start = (bf16[768,512]{1,0:T(8,128)(2,1)S(1)}, bf16[768,512]{1,0:T(8,128)(2,1)}, u32[]{:S(2)}) copy-start(bf16[768,512]{1,0:T(8,128)(2,1)} %param.9) | copy-start | bytes 2359300
  11.0 17.6 %copy-start.6 = (s32[64]{0:T(128)S(1)}, s32[64]{0:T(128)}, u32[]{:S(2)}) copy-start(s32[64]{0:T(128)} %param.7) | copy-start | bytes 772
  11.0 17.6 %copy-start.9 = (s32[64]{0:T(128)S(1)}, s32[64]{0:T(128)}, u32[]{:S(2)}) copy-start(s32[64]{0:T(128)} %param.8) | copy-start | bytes 772
  11.0 124.2 %all-to-all-start = ((bf16[24,64,768]{2,0,1:T(8,128)(2,1)}), bf16[24,64,768]{2,0,1:T(8,128)(2,1)}, u32[]{:S(2)}, u32[]{:S(2)}) async-start(bf16[24,64,768]{2,0,1:T(8,128)(2,1)} %copy.19), calls=%async_computation | async-start | bytes 4718592 | tf_op jit(solution)/shard_map/all_to_all | solution.py:46
  28.5 547.0 %all-reduce.3.cloned.1.call-start = ((), (), s32[]{:S(2)}) async-start(), calls=%async_computation.1 | async-start | bytes 4194304 | tf_op jit(solution)/shard_map/psum | solution.py:61
  138.5 13.2 %collective-permute-start = (bf16[512,768]{1,0:T(8,128)(2,1)S(1)}, bf16[512,768]{1,0:T(8,128)(2,1)S(1)}, u32[]{:S(2)}, u32[]{:S(2)}) collective-permute-start(bf16[512,768]{1,0:T(8,128)(2,1)S(1)} %fusion.5), channel_id=1, source_target_pairs={{0,8},{8,16},{16,24},{24,32},{32,40},{40,48},{48,56},{56,64},{64,7... | collective-permute-start | bytes 2359304 | tf_op jit(solution)/shard_map/ppermute | solution.py:11
  151.7 8.6 %copy-start.1 = (bf16[512,768]{1,0:T(8,128)(2,1)}, bf16[512,768]{1,0:T(8,128)(2,1)S(1)}, u32[]{:S(2)}) copy-start(bf16[512,768]{1,0:T(8,128)(2,1)S(1)} %collective-permute-done) | copy-start | bytes 2359300
  151.7 13.9 %collective-permute-start.1 = (bf16[512,768]{1,0:T(8,128)(2,1)S(1)}, bf16[512,768]{1,0:T(8,128)(2,1)}, u32[]{:S(2)}, u32[]{:S(2)}) collective-permute-start(bf16[512,768]{1,0:T(8,128)(2,1)S(1)} %collective-permute-done), channel_id=1, source_target_pairs={{0,8},{8,16},{16,24},{24,32},{32,40},{40,48},{48,56},{56,64},{64,7... | collective-permute-start | bytes 2359304 | tf_op jit(solution)/shard_map/ppermute | solution.py:11
  165.6 22.2 %collective-permute-start.2 = (bf16[512,768]{1,0:T(8,128)(2,1)}, bf16[512,768]{1,0:T(8,128)(2,1)S(1)}, u32[]{:S(2)}, u32[]{:S(2)}) collective-permute-start(bf16[512,768]{1,0:T(8,128)(2,1)} %collective-permute-done.1), channel_id=1, source_target_pairs={{0,8},{8,16},{16,24},{24,32},{32,40},{40,48},{48,56},{56,64},{64,7... | collective-permute-start | bytes 2359304 | tf_op jit(solution)/shard_map/ppermute | solution.py:11
  192.0 0.7 copy-start.4
  192.0 383.5 %copy-start.5 = (f32[512]{0:T(512)S(1)}, f32[512]{0:T(512)}, u32[]{:S(2)}) copy-start(f32[512]{0:T(512)} %param.11) | copy-start | bytes 6148
  575.5 3.3 copy-start.2
  575.5 3.3 copy-start.8
  578.8 2.2 copy-start.7
  581.0 3.2 copy-start.3
Sparse Core Ops, SparseCore 0:
  192.1 383.2 all-reduce.2
where the time goes:
time: 595 us; the launch traced here: 594 us
  waiting for transfers between devices  506 us (85%)
  starting transfers between devices  30.2 us (5%)
  matrix products  18.9 us (3%)
  local copies, waits for them, and re-layouts  16.1 us (3%)
  between operations  13.7 us (2%)
  other arithmetic  9.85 us (2%)
    psum x1, waiting for transfers between devices, shards(): lax.psum(partial_value.astype(jnp.bfloat16), 'aux').astype(jnp.float32)  382 us
    all_to_all x1, waiting for transfers between devices, shards(): lax.all_to_all(half_blocks, 'occ', split_axis=1, concat_axis=0, tiled=True)  101 us
    ppermute x3, waiting for transfers between devices, shifted(): lax.ppermute(value, axis, [(i, (i + by) % devices) for i in range(devices)])  22.9 us
    all_to_all x1, starting transfers between devices, shards(): lax.all_to_all(half_blocks, 'occ', split_axis=1, concat_axis=0, tiled=True)  17.5 us
    ppermute x3, starting transfers between devices, shifted(): lax.ppermute(value, axis, [(i, (i + by) % devices) for i in range(devices)])  12.7 us
    dot_general x4, matrix products, shards(): jnp.dot(amplitudes, other_tile, preferred_element_type=jnp.float32)  12 us
  transfers between devices with their start and end apart: 5, of which 5 were waited for; matrix products, arithmetic and copies ran while one was open for 3% of the time, Pallas kernels for 0%

commit v1 on v0

v1 whole, which is shorter than its diff:
```python
import functools

import jax
import jax.numpy as jnp
from jax import lax
from jax.experimental import pallas as pl
from jax.experimental.pallas import tpu as pltpu
from jax.sharding import PartitionSpec as P


XS = 4
ZS = 2


def shifted(value, axis, by):
    devices = lax.axis_size(axis)
    return lax.ppermute(value, axis, [(i, (i + by) % devices) for i in range(devices)])


def exchanged_x(value):
    groups = [[x * ZS + z for x in range(XS)] for z in range(ZS)]
    return lax.all_to_all(value, "aux", 0, 0, axis_index_groups=groups, tiled=True)


def swapped_z(value):
    perm = [(x * ZS + z, x * ZS + 1 - z) for x in range(XS) for z in range(ZS)]
    return lax.ppermute(value, "aux", perm)


def ao_layout(block_rows, block_order, maxrows):
    device_count = block_rows.shape[0]
    matches = block_order[:, None] == jnp.arange(device_count, dtype=jnp.int32)[None, :]
    ordered = jnp.sum(jnp.where(matches, block_rows[None, :], 0), axis=1)
    before = jnp.cumsum(ordered) - ordered
    starts = jnp.sum(jnp.where(matches, before[:, None], 0), axis=0)
    offset = jnp.arange(maxrows, dtype=jnp.int32)
    in_block = offset[None, :] < block_rows[:, None]
    target = starts[:, None] + offset[None, :]
    return (in_block, target)


def build_table(block_rows, block_order, ao_to_virt, maxrows):
    in_block, target = ao_layout(block_rows, block_order, maxrows)
    row_index = jnp.where(in_block, target, 0).reshape(-1)
    ao_rows = jnp.take(ao_to_virt, row_index, axis=0)
    return jnp.where(in_block.reshape(-1, 1), ao_rows, jnp.zeros_like(ao_rows))


def contract_rows(ao_table, received):
    return lax.dot_general(
        ao_table, received, (((0,), (0,)), ((), ())), preferred_element_type=jnp.float32
    ).astype(jnp.bfloat16)


NT = (((1,), (1,)), ((), ()))
IN_VMEM = pl.BlockSpec(memory_space=pltpu.VMEM)
IN_SMEM = pl.BlockSpec(memory_space=pltpu.SMEM)


def grant(mib):
    return pltpu.CompilerParams(vmem_limit_bytes=mib << 20)


def pair_kernel(own_ref, *refs):
    others, out_ref = refs[:-1], refs[-1]
    copies, _, rows, _ = out_ref.shape
    for step in range(copies):
        block = pl.ds(step * rows, rows)
        for k, other_ref in enumerate(others):
            direct = lax.dot_general(
                own_ref[block, :], other_ref[...], NT, preferred_element_type=jnp.float32
            )
            crossed = lax.dot_general(
                other_ref[block, :], own_ref[...], NT, preferred_element_type=jnp.float32
            )
            out_ref[step, k] = (2.0 * direct - crossed).astype(out_ref.dtype)


def pair_blocks(own, others):
    vt, columns = own.shape
    count = len(others)
    return pl.pallas_call(
        pair_kernel,
        out_shape=jax.ShapeDtypeStruct((XS, count, vt // XS, vt), jnp.bfloat16),
        in_specs=[IN_VMEM] * (1 + count),
        out_specs=IN_VMEM,
        compiler_params=grant(4 + 2 * count),
        cost_estimate=pl.CostEstimate(
            flops=4 * count * vt * vt * columns,
            bytes_accessed=2 * (1 + count) * vt * columns + 2 * count * vt * vt,
            transcendentals=0,
        ),
    )(own, *others)


def sum_kernel(blocks_ref, out_ref):
    total = blocks_ref[0].astype(jnp.float32)
    for step in range(1, blocks_ref.shape[0]):
        total = total + blocks_ref[step].astype(jnp.float32)
    out_ref[...] = total.astype(out_ref.dtype)


def sum_of(blocks):
    return pl.pallas_call(
        sum_kernel,
        out_shape=jax.ShapeDtypeStruct(blocks.shape[1:], jnp.bfloat16),
        in_specs=[IN_VMEM],
        out_specs=IN_VMEM,
        compiler_params=grant(4),
        cost_estimate=pl.CostEstimate(
            flops=blocks.size, bytes_accessed=3 * blocks.size, transcendentals=0
        ),
    )(blocks)


def amplitude_kernel(steps, place_ref, energy_ref, column_ref, row_ref, one_ref, two_ref, out_ref):
    copies, _, rows, _ = out_ref.shape
    occupied = energy_ref.shape[0]
    position = place_ref[0]
    block = pl.ds(pl.multiple_of(place_ref[1] * rows, rows), rows)
    both = column_ref[block, :] + row_ref[...]
    for k, step in enumerate(steps):
        partner = lax.rem(position + occupied - step, occupied)
        gap = both - energy_ref[position] - energy_ref[partner]
        merged = one_ref[k].astype(jnp.float32) + two_ref[k].astype(jnp.float32)
        amplitude = (merged / gap).astype(out_ref.dtype)
        for copy in range(copies):
            out_ref[copy, k] = amplitude


def amplitude_of(steps, place, energies, column, row, one, two):
    return pl.pallas_call(
        functools.partial(amplitude_kernel, steps),
        out_shape=jax.ShapeDtypeStruct((XS,) + one.shape, jnp.bfloat16),
        in_specs=[IN_SMEM] * 2 + [IN_VMEM] * 4,
        out_specs=IN_VMEM,
        compiler_params=grant(6),
        cost_estimate=pl.CostEstimate(
            flops=6 * one.size, bytes_accessed=12 * one.size, transcendentals=0
        ),
    )(place, energies, column, row, one, two)


def density_kernel(counts, *refs):
    amplitudes, tiles = refs[: len(counts)], refs[len(counts) : len(counts) + sum(counts)]
    rest = refs[len(counts) + sum(counts) :]
    out_ref = rest[-1]
    steps, _, rows, _ = amplitudes[0].shape
    pairs = [(ref, k) for ref, count in zip(amplitudes, counts) for k in range(count)]
    for step in range(steps):
        block = pl.ds(step * rows, rows)
        total = rest[0][block, :] if len(rest) > 1 else None
        for (ref, k), tile in zip(pairs, tiles):
            term = jnp.dot(ref[step, k], tile[...], preferred_element_type=jnp.float32)
            total = term if total is None else total + term
        out_ref[block, :] = total


def density_of(amplitudes, tiles, so_far=None):
    counts = [a.shape[1] for a in amplitudes]
    count = sum(counts)
    vt, columns = tiles[0].shape
    args = list(amplitudes) + list(tiles)
    aliases = {}
    if so_far is not None:
        aliases = {len(args): 0}
        args.append(so_far)
    return pl.pallas_call(
        functools.partial(density_kernel, counts),
        out_shape=jax.ShapeDtypeStruct((vt, columns), jnp.float32),
        in_specs=[IN_VMEM] * len(args),
        out_specs=IN_VMEM,
        compiler_params=grant(12),
        input_output_aliases=aliases,
        cost_estimate=pl.CostEstimate(
            flops=2 * count * vt * vt * columns,
            bytes_accessed=4 * vt * columns + count * (2 * vt * columns + 2 * vt * vt),
            transcendentals=0,
        ),
    )(*args)


GROUPS = ((0,), (1, 2), (3,))


def shards(half_blocks, block_rows, block_order, ao_to_virt, occ_energy, virt_energy):
    maxrows = half_blocks.shape[0]
    place = jnp.stack([lax.axis_index("occ"), lax.axis_index("aux") // ZS]).astype(jnp.int32)
    column, row = virt_energy[:, None], virt_energy[None, :]
    ao_table = build_table(block_rows, block_order, ao_to_virt, maxrows)
    own_tile = contract_rows(
        ao_table,
        lax.all_to_all(half_blocks, "occ", split_axis=1, concat_axis=0, tiled=True)[:, 0, :],
    )
    tiles = [own_tile, shifted(own_tile, "occ", 1), shifted(own_tile, "occ", 2)]
    tiles.append(shifted(tiles[2], "occ", 1))
    amplitudes = []
    for steps in GROUPS:
        blocks = pair_blocks(own_tile, [tiles[k] for k in steps])
        received = exchanged_x(blocks)
        part = sum_of(received)
        other = swapped_z(part)
        amplitude = amplitude_of(steps, place, occ_energy, column, row, part, other)
        amplitudes.append(exchanged_x(amplitude))
    density = density_of(amplitudes[:2], tiles[:3])
    return density_of(amplitudes[2:], tiles[3:], density)[None]


def solution(mesh):
    return jax.shard_map(
        shards,
        mesh=mesh,
        in_specs=(P("occ", None, "aux"), P(), P(), P(), P(), P()),
        out_specs=P("occ", None, "aux"),
        check_vma=False,
    )
```

time: 595 us -> 286 us (0.48)
  waiting for transfers between devices: 506 us -> 159 us
  starting transfers between devices: 30.2 us -> 68 us
  Pallas kernels: 0 us -> 22.9 us
  matrix products: 18.9 us -> 3.36 us
  blocking collectives: 0 us -> 13.6 us
  between operations: 13.7 us -> 0.32 us
  other arithmetic: 9.85 us -> 0.78 us
    psum x1 -> x0, waiting for transfers between devices: 382 us -> none  [shards(): lax.psum(partial_value.astype(jnp.bfloat16), 'aux').astype(jnp.float32)]
    ppermute x0 -> x3, waiting for transfers between devices: none -> 45.3 us  [swapped_z(): return lax.ppermute(value, 'aux', perm)]
    pallas_call x0 -> x11, Pallas kernels: none -> 22.9 us  [the longest x3 11 us: pair_blocks(): pl.pallas_call(pair_kernel, out_shape=jax.ShapeDtypeStruct((XS, count, vt...]
    ppermute x3, waiting for transfers between devices: 22.9 us -> 0.01 us  [shifted(): lax.ppermute(value, axis, [(i, (i + by) % devices) for i in range(devices)])]
    ppermute x0 -> x3, starting transfers between devices: none -> 21 us  [swapped_z(): return lax.ppermute(value, 'aux', perm)]
    all_to_all x0 -> x5, starting transfers between devices: none -> 19.9 us  [exchanged_x(): lax.all_to_all(value, 'aux', 0, 0, axis_index_groups=groups, tiled=True)]
    dot_general x8 -> x0, matrix products: 15.5 us -> none  [the longest x4 12 us: shards(): jnp.dot(amplitudes, other_tile, preferred_element_type=jnp.float32)]
    all_to_all x0 -> x1, blocking collectives: none -> 13.6 us  [exchanged_x(): lax.all_to_all(value, 'aux', 0, 0, axis_index_groups=groups, tiled=True)]
  transfers between devices with their start and end apart: 5 -> 12, of which waited for: 5 -> 7; matrix products, arithmetic and copies ran while one was open for 3% -> 2% of each run, Pallas kernels for 0% -> 7%
where the time goes in v1:
time: 286 us; the launch traced here: 282 us
  waiting for transfers between devices  159 us (56%)
  starting transfers between devices  68 us (24%)
  Pallas kernels  22.9 us (8%)
  local copies, waits for them, and re-layouts  13.8 us (5%)
  blocking collectives  13.6 us (5%)
  matrix products  3.36 us (1%)
    all_to_all x1, waiting for transfers between devices, shards(): lax.all_to_all(half_blocks, 'occ', split_axis=1, concat_axis=0, tiled=True)  101 us
    ppermute x3, waiting for transfers between devices, swapped_z(): return lax.ppermute(value, 'aux', perm)  45.3 us
    ppermute x3, starting transfers between devices, swapped_z(): return lax.ppermute(value, 'aux', perm)  21 us
    all_to_all x5, starting transfers between devices, exchanged_x(): lax.all_to_all(value, 'aux', 0, 0, axis_index_groups=groups, tiled=True)  19.9 us
    all_to_all x1, starting transfers between devices, shards(): lax.all_to_all(half_blocks, 'occ', split_axis=1, concat_axis=0, tiled=True)  17.5 us
    all_to_all x1, blocking collectives, exchanged_x(): lax.all_to_all(value, 'aux', 0, 0, axis_index_groups=groups, tiled=True)  13.6 us
    all_to_all x5, waiting for transfers between devices, exchanged_x(): lax.all_to_all(value, 'aux', 0, 0, axis_index_groups=groups, tiled=True)  13 us
    pallas_call x3, Pallas kernels, pair_blocks(): pl.pallas_call(pair_kernel, out_shape=jax.ShapeDtypeStruct((XS, count, vt...  11 us
  transfers between devices with their start and end apart: 12, of which 7 were waited for; matrix products, arithmetic and copies ran while one was open for 2% of the time, Pallas kernels for 7%

profile of v1, /device:TPU:1, one launch (start us, length us, event | category | flops | bytes accessed | tf_op | source)
XLA Modules:
  0.0 281.9 jit_solution(12838559302823847182)
XLA Ops:
  0.0 4.5 %copy.15 = bf16[24,64,768]{2,0,1:T(8,128)(2,1)} copy(bf16[24,64,768]{2,1,0:T(8,128)(2,1)} %param.6) | data formatting | bytes 4718592 | tf_op args[0]
  4.5 17.5 %all-to-all-start = ((bf16[24,64,768]{2,0,1:T(8,128)(2,1)}), bf16[24,64,768]{2,0,1:T(8,128)(2,1)}, u32[]{:S(2)}, u32[]{:S(2)}) async-start(bf16[24,64,768]{2,0,1:T(8,128)(2,1)} %copy.15), calls=%async_computation | async-start | bytes 4718592 | tf_op jit(solution)/shard_map/all_to_all | solution.py:193
  23.1 4.8 %gather_fusion = bf16[1536,512]{1,0:T(8,128)(2,1)S(1)} fusion(bf16[768,512]{1,0:T(8,128)(2,1)S(1)} %copy-done, s32[2048]{0:T(1024)S(1)} %pad_clamp_fusion), kind=kCustom, calls=%fused_computation | custom fusion | bytes 3151872 | tf_op jit(solution)/shard_map/jit(_take)/gather | solution.py:45
  28.0 100.7 %all-to-all-done = bf16[24,64,768]{2,0,1:T(8,128)(2,1)} async-done(((bf16[24,64,768]{2,0,1:T(8,128)(2,1)}), bf16[24,64,768]{2,0,1:T(8,128)(2,1)}, u32[]{:S(2)}, u32[]{:S(2)}) %all-to-all-start) | async-done | bytes 2359328 | tf_op jit(solution)/shard_map/all_to_all | solution.py:193
  128.6 3.4 %fusion.5.own_ref.refs_0_.refs_2_ = bf16[512,768]{1,0:T(8,128)(2,1)S(1)} fusion(bf16[1536,768]{1,0:T(8,128)(2,1)} %bitcast.7, bf16[1536,512]{1,0:T(8,128)(2,1)S(1)} %gather_fusion, pred[1536]{0:T(1024)(128)(4,1)S(1)} %compare_and_fusion, pred[1536]{0:T(1024)(128)(4,1)S(1)} %lt.52), kind=kOutput, calls=%fused_computation.6 | convolution fusion | flops 1209925632 | bytes 4721664 | tf_op jit(solution)/shard_map/dot_general | solution.py:50
  132.0 3.1 %collective-permute-start = (bf16[512,768]{1,0:T(8,128)(2,1)S(1)}, bf16[512,768]{1,0:T(8,128)(2,1)}, u32[]{:S(2)}, u32[]{:S(2)}) collective-permute-start(bf16[512,768]{1,0:T(8,128)(2,1)S(1)} %fusion.5.own_ref.refs_0_.refs_2_), channel_id=1, source_target_pairs={{0,16},{8,24},{16,32},{24,40},{32,48},{40,56},{48,64},{56,72},{64,... | collective-permute-start | bytes 2359304 | tf_op jit(solution)/shard_map/ppermute | solution.py:17
  135.1 4.5 %collective-permute-start.4 = (bf16[512,768]{1,0:T(8,128)(2,1)S(1)}, bf16[512,768]{1,0:T(8,128)(2,1)S(1)}, u32[]{:S(2)}, u32[]{:S(2)}) collective-permute-start(bf16[512,768]{1,0:T(8,128)(2,1)S(1)} %fusion.5.own_ref.refs_0_.refs_2_), channel_id=1, source_target_pairs={{0,8},{8,16},{16,24},{24,32},{32,40},{40,48},{48,56},{56,64},{64,7... | collective-permute-start | bytes 2359304 | tf_op jit(solution)/shard_map/ppermute | solution.py:17
  139.6 2.1 shard_map.67
  141.8 13.6 %all_to_all.45.blocks_ref = bf16[4,1,128,512]{3,2,1,0:T(8,128)(2,1)S(1)} all-to-all(bf16[4,1,128,512]{3,2,1,0:T(8,128)(2,1)S(1)} %shard_map.67), channel_id=1, replica_groups={{0,2,4,6},{1,3,5,7},{8,10,12,14},{9,11,13,15},{16,18,20,22},{17,19,21,2..., dimensions={0} | all-to-all | bytes 1048576 | tf_op jit(solution)/shard_map/all_to_all | solution.py:22
  155.5 8.0 %collective-permute-start.3 = (bf16[1,128,512]{2,1,0:T(8,128)(2,1)S(1)}, bf16[1,128,512]{2,1,0:T(8,128)(2,1)S(1)}, u32[]{:S(2)}, u32[]{:S(2)}) collective-permute-start(bf16[1,128,512]{2,1,0:T(8,128)(2,1)S(1)} %shard_map.68.one_ref), channel_id=1, source_target_pairs={{0,1},{1,0},{2,3},{3,2},{4,5},{5,4},{6,7},{7,6},{8,9},{9,8},{10,11... | collective-permute-start | bytes 393224 | tf_op jit(solution)/shard_map/ppermute | solution.py:27
  163.7 15.3 %collective-permute-done.3.two_ref = bf16[1,128,512]{2,1,0:T(8,128)(2,1)S(1)} collective-permute-done((bf16[1,128,512]{2,1,0:T(8,128)(2,1)S(1)}, bf16[1,128,512]{2,1,0:T(8,128)(2,1)S(1)}, u32[]{:S(2)}, u32[]{:S(2)}) %collective-permute-start.3) | collective-permute-done | bytes 131104 | tf_op jit(solution)/shard_map/ppermute | solution.py:27
  179.0 1.5 shard_map.69
  180.5 3.5 %all-to-all-start.4 = ((bf16[4,1,128,512]{3,2,1,0:T(8,128)(2,1)}), bf16[4,1,128,512]{3,2,1,0:T(8,128)(2,1)S(1)}, u32[]{:S(2)}, u32[]{:S(2)}) async-start(bf16[4,1,128,512]{3,2,1,0:T(8,128)(2,1)} %shard_map.69), calls=%async_computation.4 | async-start | bytes 1048576 | tf_op jit(solution)/shard_map/all_to_all | solution.py:22
  184.0 2.0 collective-permute-start.1
  186.0 5.6 %shard_map.70 = bf16[4,2,128,512]{3,2,1,0:T(8,128)(2,1)S(1)} custom-call(bf16[512,768]{1,0:T(8,128)(2,1)S(1)} %fusion.5.own_ref.refs_0_.refs_2_, bf16[512,768]{1,0:T(8,128)(2,1)S(1)} %collective-permute-done.4.refs_0_.refs_3_, bf16[512,768]{1,0:T(8,128)(2,1)} %collective-permute-done.refs_1_.refs_4_), custom_call_target="tpu_custom_call" | custom-call | flops 1610612736 | bytes 3407872 | tf_op jit(solution)/shard_map/pallas_call | solution.py:82
  193.0 4.0 %all-to-all-start.5 = ((bf16[4,2,128,512]{3,2,1,0:T(8,128)(2,1)}), bf16[4,2,128,512]{3,2,1,0:T(8,128)(2,1)S(1)}, u32[]{:S(2)}, u32[]{:S(2)}) async-start(bf16[4,2,128,512]{3,2,1,0:T(8,128)(2,1)} %copy-done.1), calls=%async_computation.5 | async-start | bytes 2097152 | tf_op jit(solution)/shard_map/all_to_all | solution.py:22
  197.0 3.3 %shard_map.64 = bf16[4,1,128,512]{3,2,1,0:T(8,128)(2,1)S(1)} custom-call(bf16[512,768]{1,0:T(8,128)(2,1)S(1)} %fusion.5.own_ref.refs_0_.refs_2_, bf16[512,768]{1,0:T(8,128)(2,1)} %collective-permute-done.1.refs_0_.refs_1_), custom_call_target="tpu_custom_call" | custom-call | flops 805306368 | bytes 2097152 | tf_op jit(solution)/shard_map/pallas_call | solution.py:82
  201.1 10.2 %all-to-all-done.5.blocks_ref = bf16[4,2,128,512]{3,2,1,0:T(8,128)(2,1)S(1)} async-done(((bf16[4,2,128,512]{3,2,1,0:T(8,128)(2,1)}), bf16[4,2,128,512]{3,2,1,0:T(8,128)(2,1)S(1)}, u32[]{:S(2)}, u32[]{:S(2)}) %all-to-all-start.5) | async-done | bytes 1048608 | tf_op jit(solution)/shard_map/all_to_all | solution.py:22
  211.3 3.5 %all-to-all-start.1 = ((bf16[4,1,128,512]{3,2,1,0:T(8,128)(2,1)}), bf16[4,1,128,512]{3,2,1,0:T(8,128)(2,1)S(1)}, u32[]{:S(2)}, u32[]{:S(2)}) async-start(bf16[4,1,128,512]{3,2,1,0:T(8,128)(2,1)} %copy-done.6), calls=%async_computation.1 | async-start | bytes 1048576 | tf_op jit(solution)/shard_map/all_to_all | solution.py:22
  214.9 5.8 %collective-permute-start.5 = (bf16[2,128,512]{2,1,0:T(8,128)(2,1)S(1)}, bf16[2,128,512]{2,1,0:T(8,128)(2,1)S(1)}, u32[]{:S(2)}, u32[]{:S(2)}) collective-permute-start(bf16[2,128,512]{2,1,0:T(8,128)(2,1)S(1)} %shard_map.71.one_ref), channel_id=1, source_target_pairs={{0,1},{1,0},{2,3},{3,2},{4,5},{5,4},{6,7},{7,6},{8,9},{9,8},{10,11... | collective-permute-start | bytes 786440 | tf_op jit(solution)/shard_map/ppermute | solution.py:27
  220.7 20.6 %collective-permute-done.5.two_ref = bf16[2,128,512]{2,1,0:T(8,128)(2,1)S(1)} collective-permute-done((bf16[2,128,512]{2,1,0:T(8,128)(2,1)S(1)}, bf16[2,128,512]{2,1,0:T(8,128)(2,1)S(1)}, u32[]{:S(2)}, u32[]{:S(2)}) %collective-permute-start.5) | collective-permute-done | bytes 262176 | tf_op jit(solution)/shard_map/ppermute | solution.py:27
  241.3 1.7 shard_map.72
  243.0 4.5 %all-to-all-start.6 = ((bf16[4,2,128,512]{3,2,1,0:T(8,128)(2,1)}), bf16[4,2,128,512]{3,2,1,0:T(8,128)(2,1)S(1)}, u32[]{:S(2)}, u32[]{:S(2)}) async-start(bf16[4,2,128,512]{3,2,1,0:T(8,128)(2,1)} %shard_map.72), calls=%async_computation.6 | async-start | bytes 2097152 | tf_op jit(solution)/shard_map/all_to_all | solution.py:22
  247.5 7.3 %collective-permute-start.2 = (bf16[1,128,512]{2,1,0:T(8,128)(2,1)S(1)}, bf16[1,128,512]{2,1,0:T(8,128)(2,1)S(1)}, u32[]{:S(2)}, u32[]{:S(2)}) collective-permute-start(bf16[1,128,512]{2,1,0:T(8,128)(2,1)S(1)} %shard_map.65.one_ref), channel_id=1, source_target_pairs={{0,1},{1,0},{2,3},{3,2},{4,5},{5,4},{6,7},{7,6},{8,9},{9,8},{10,11... | collective-permute-start | bytes 393224 | tf_op jit(solution)/shard_map/ppermute | solution.py:27
  254.8 9.5 %collective-permute-done.2.two_ref = bf16[1,128,512]{2,1,0:T(8,128)(2,1)S(1)} collective-permute-done((bf16[1,128,512]{2,1,0:T(8,128)(2,1)S(1)}, bf16[1,128,512]{2,1,0:T(8,128)(2,1)S(1)}, u32[]{:S(2)}, u32[]{:S(2)}) %collective-permute-start.2) | collective-permute-done | bytes 131104 | tf_op jit(solution)/shard_map/ppermute | solution.py:27
  264.3 1.5 shard_map.66
  265.8 4.5 %all-to-all-start.2 = ((bf16[4,1,128,512]{3,2,1,0:T(8,128)(2,1)}), bf16[4,1,128,512]{3,2,1,0:T(8,128)(2,1)S(1)}, u32[]{:S(2)}, u32[]{:S(2)}) async-start(bf16[4,1,128,512]{3,2,1,0:T(8,128)(2,1)} %shard_map.66), calls=%async_computation.2 | async-start | bytes 1048576 | tf_op jit(solution)/shard_map/all_to_all | solution.py:22
  270.3 1.1 copy-done.3
  271.5 1.1 copy-done.5
  272.6 3.7 %shard_map.73.refs_2_ = f32[512,768]{1,0:T(8,128)} custom-call(bf16[4,1,128,512]{3,2,1,0:T(8,128)(2,1)S(1)} %all-to-all-done.4.refs_0_, bf16[4,2,128,512]{3,2,1,0:T(8,128)(2,1)S(1)} %all-to-all-done.6.refs_1_, bf16[512,768]{1,0:T(8,128)(2,1)S(1)} %copy-done.3, bf16[512,768]{1,0:T(8,128)(2,1)S(1)} %copy-done.5, ...), custom_call_target="tpu_custom_call" | custom-call | flops 1207959552 | bytes 5505024 | tf_op jit(solution)/shard_map/pallas_call | solution.py:168
  276.2 2.2 all-to-all-done.2.refs_0_
  278.5 3.4 %shard_map.74 = f32[512,768]{1,0:T(8,128)} custom-call(bf16[4,1,128,512]{3,2,1,0:T(8,128)(2,1)S(1)} %all-to-all-done.2.refs_0_, bf16[512,768]{1,0:T(8,128)(2,1)} %collective-permute-done.1.refs_0_.refs_1_, f32[512,768]{1,0:T(8,128)} %shard_map.73.refs_2_), custom_call_target="tpu_custom_call", output_to_operand_aliasing={{}: (2, {})} | custom-call | flops 402653184 | bytes 2883584 | tf_op jit(solution)/shard_map/pallas_call | solution.py:168
  (45 shorter events, 3.9 us)
Async XLA Ops:
  0.0 23.1 %copy-start = (bf16[768,512]{1,0:T(8,128)(2,1)S(1)}, bf16[768,512]{1,0:T(8,128)(2,1)}, u32[]{:S(2)}) copy-start(bf16[768,512]{1,0:T(8,128)(2,1)} %param.9) | copy-start | bytes 2359300
  4.5 17.5 %copy-start.9 = (s32[64]{0:T(128)S(1)}, s32[64]{0:T(128)}, u32[]{:S(2)}) copy-start(s32[64]{0:T(128)} %param.7) | copy-start | bytes 772
  4.5 17.5 %copy-start.10 = (s32[64]{0:T(128)S(1)}, s32[64]{0:T(128)}, u32[]{:S(2)}) copy-start(s32[64]{0:T(128)} %param.8) | copy-start | bytes 772
  4.5 124.2 %all-to-all-start = ((bf16[24,64,768]{2,0,1:T(8,128)(2,1)}), bf16[24,64,768]{2,0,1:T(8,128)(2,1)}, u32[]{:S(2)}, u32[]{:S(2)}) async-start(bf16[24,64,768]{2,0,1:T(8,128)(2,1)} %copy.15), calls=%async_computation | async-start | bytes 4718592 | tf_op jit(solution)/shard_map/all_to_all | solution.py:193
  132.0 65.0 %copy-start.2 = (bf16[512,768]{1,0:T(8,128)(2,1)}, bf16[512,768]{1,0:T(8,128)(2,1)S(1)}, u32[]{:S(2)}) copy-start(bf16[512,768]{1,0:T(8,128)(2,1)S(1)} %fusion.5.own_ref.refs_0_.refs_2_) | copy-start | bytes 2359300
  132.0 52.0 %collective-permute-start = (bf16[512,768]{1,0:T(8,128)(2,1)S(1)}, bf16[512,768]{1,0:T(8,128)(2,1)}, u32[]{:S(2)}, u32[]{:S(2)}) collective-permute-start(bf16[512,768]{1,0:T(8,128)(2,1)S(1)} %fusion.5.own_ref.refs_0_.refs_2_), channel_id=1, source_target_pairs={{0,16},{8,24},{16,32},{24,40},{32,48},{40,56},{48,64},{56,72},{64,... | collective-permute-start | bytes 2359304 | tf_op jit(solution)/shard_map/ppermute | solution.py:17
  135.1 50.9 %collective-permute-start.4 = (bf16[512,768]{1,0:T(8,128)(2,1)S(1)}, bf16[512,768]{1,0:T(8,128)(2,1)S(1)}, u32[]{:S(2)}, u32[]{:S(2)}) collective-permute-start(bf16[512,768]{1,0:T(8,128)(2,1)S(1)} %fusion.5.own_ref.refs_0_.refs_2_), channel_id=1, source_target_pairs={{0,8},{8,16},{16,24},{24,32},{32,40},{40,48},{48,56},{56,64},{64,7... | collective-permute-start | bytes 2359304 | tf_op jit(solution)/shard_map/ppermute | solution.py:17
  141.8 21.7 %copy-start.7 = (f32[512]{0:T(512)S(1)}, f32[512]{0:T(512)}, u32[]{:S(2)}) copy-start(f32[512]{0:T(512)} %param.11) | copy-start | bytes 6148
  141.8 37.2 %copy-start.8 = (f32[64]{0:T(128)S(1)}, f32[64]{0:T(128)}, u32[]{:S(2)}) copy-start(f32[64]{0:T(128)} %energy_ref.5) | copy-start | bytes 772
  155.5 23.5 %collective-permute-start.3 = (bf16[1,128,512]{2,1,0:T(8,128)(2,1)S(1)}, bf16[1,128,512]{2,1,0:T(8,128)(2,1)S(1)}, u32[]{:S(2)}, u32[]{:S(2)}) collective-permute-start(bf16[1,128,512]{2,1,0:T(8,128)(2,1)S(1)} %shard_map.68.one_ref), channel_id=1, source_target_pairs={{0,1},{1,0},{2,3},{3,2},{4,5},{5,4},{6,7},{7,6},{8,9},{9,8},{10,11... | collective-permute-start | bytes 393224 | tf_op jit(solution)/shard_map/ppermute | solution.py:27
  180.5 12.5 %all-to-all-start.4 = ((bf16[4,1,128,512]{3,2,1,0:T(8,128)(2,1)}), bf16[4,1,128,512]{3,2,1,0:T(8,128)(2,1)S(1)}, u32[]{:S(2)}, u32[]{:S(2)}) async-start(bf16[4,1,128,512]{3,2,1,0:T(8,128)(2,1)} %shard_map.69), calls=%async_computation.4 | async-start | bytes 1048576 | tf_op jit(solution)/shard_map/all_to_all | solution.py:22
  184.0 13.0 %collective-permute-start.1 = (bf16[512,768]{1,0:T(8,128)(2,1)}, bf16[512,768]{1,0:T(8,128)(2,1)}, u32[]{:S(2)}, u32[]{:S(2)}) collective-permute-start(bf16[512,768]{1,0:T(8,128)(2,1)} %collective-permute-done.refs_1_.refs_4_), channel_id=1, source_target_pairs={{0,8},{8,16},{16,24},{24,32},{32,40},{40,48},{48,56},{56,64},{64,7... | collective-permute-start | bytes 2359304 | tf_op jit(solution)/shard_map/ppermute | solution.py:17
  186.0 5.6 %copy-start.4 = (bf16[512,768]{1,0:T(8,128)(2,1)}, bf16[512,768]{1,0:T(8,128)(2,1)S(1)}, u32[]{:S(2)}) copy-start(bf16[512,768]{1,0:T(8,128)(2,1)S(1)} %collective-permute-done.4.refs_0_.refs_3_) | copy-start | bytes 2359300
  191.5 1.0 copy-start.1
  193.0 18.3 %all-to-all-start.5 = ((bf16[4,2,128,512]{3,2,1,0:T(8,128)(2,1)}), bf16[4,2,128,512]{3,2,1,0:T(8,128)(2,1)S(1)}, u32[]{:S(2)}, u32[]{:S(2)}) async-start(bf16[4,2,128,512]{3,2,1,0:T(8,128)(2,1)} %copy-done.1), calls=%async_computation.5 | async-start | bytes 2097152 | tf_op jit(solution)/shard_map/all_to_all | solution.py:22
  200.3 0.8 copy-start.6
  211.3 31.7 %all-to-all-start.1 = ((bf16[4,1,128,512]{3,2,1,0:T(8,128)(2,1)}), bf16[4,1,128,512]{3,2,1,0:T(8,128)(2,1)S(1)}, u32[]{:S(2)}, u32[]{:S(2)}) async-start(bf16[4,1,128,512]{3,2,1,0:T(8,128)(2,1)} %copy-done.6), calls=%async_computation.1 | async-start | bytes 1048576 | tf_op jit(solution)/shard_map/all_to_all | solution.py:22
  214.9 26.4 %collective-permute-start.5 = (bf16[2,128,512]{2,1,0:T(8,128)(2,1)S(1)}, bf16[2,128,512]{2,1,0:T(8,128)(2,1)S(1)}, u32[]{:S(2)}, u32[]{:S(2)}) collective-permute-start(bf16[2,128,512]{2,1,0:T(8,128)(2,1)S(1)} %shard_map.71.one_ref), channel_id=1, source_target_pairs={{0,1},{1,0},{2,3},{3,2},{4,5},{5,4},{6,7},{7,6},{8,9},{9,8},{10,11... | collective-permute-start | bytes 786440 | tf_op jit(solution)/shard_map/ppermute | solution.py:27
  243.0 22.8 %all-to-all-start.6 = ((bf16[4,2,128,512]{3,2,1,0:T(8,128)(2,1)}), bf16[4,2,128,512]{3,2,1,0:T(8,128)(2,1)S(1)}, u32[]{:S(2)}, u32[]{:S(2)}) async-start(bf16[4,2,128,512]{3,2,1,0:T(8,128)(2,1)} %shard_map.72), calls=%async_computation.6 | async-start | bytes 2097152 | tf_op jit(solution)/shard_map/all_to_all | solution.py:22
  247.5 16.8 %collective-permute-start.2 = (bf16[1,128,512]{2,1,0:T(8,128)(2,1)S(1)}, bf16[1,128,512]{2,1,0:T(8,128)(2,1)S(1)}, u32[]{:S(2)}, u32[]{:S(2)}) collective-permute-start(bf16[1,128,512]{2,1,0:T(8,128)(2,1)S(1)} %shard_map.65.one_ref), channel_id=1, source_target_pairs={{0,1},{1,0},{2,3},{3,2},{4,5},{5,4},{6,7},{7,6},{8,9},{9,8},{10,11... | collective-permute-start | bytes 393224 | tf_op jit(solution)/shard_map/ppermute | solution.py:27
  265.8 12.7 %all-to-all-start.2 = ((bf16[4,1,128,512]{3,2,1,0:T(8,128)(2,1)}), bf16[4,1,128,512]{3,2,1,0:T(8,128)(2,1)S(1)}, u32[]{:S(2)}, u32[]{:S(2)}) async-start(bf16[4,1,128,512]{3,2,1,0:T(8,128)(2,1)} %shard_map.66), calls=%async_computation.2 | async-start | bytes 1048576 | tf_op jit(solution)/shard_map/all_to_all | solution.py:22
  270.3 1.1 copy-start.3
  271.4 1.1 copy-start.5

commit v2 on v1

--- a/solution.py
+++ b/solution.py
@@ -1,4 +1,5 @@
 import functools
+import math
 
 import jax
 import jax.numpy as jnp
@@ -10,6 +11,9 @@
 
 XS = 4
 ZS = 2
+PLANE = 8
+DIRECT = 8
+STEADY = 80
 
 
 def shifted(value, axis, by):
@@ -27,28 +31,55 @@
     return lax.ppermute(value, "aux", perm)
 
 
-def ao_layout(block_rows, block_order, maxrows):
-    device_count = block_rows.shape[0]
-    matches = block_order[:, None] == jnp.arange(device_count, dtype=jnp.int32)[None, :]
+def crossed(value, mask):
+    devices = lax.axis_size("occ")
+    return lax.ppermute(value, "occ", [(i, i ^ mask) for i in range(devices)])
+
+
+def picked(table, index):
+    hot = index[:, None] == jnp.arange(table.shape[0], dtype=jnp.int32)[None, :]
+    hot = hot.reshape(hot.shape + (1,) * (table.ndim - 1))
+    return jnp.sum(jnp.where(hot, table[None], 0), axis=1)
+
+
+def exclusive_sum(value):
+    place = jnp.arange(value.shape[-1], dtype=jnp.int32)
+    ahead = place[None, :] < place[:, None]
+    return jnp.sum(jnp.where(ahead, value[..., None, :], 0), axis=-1)
+
+
+def row_layout(block_rows, block_order, maxrows, plane, in_plane):
+    devices = block_rows.shape[0]
+    numbers = jnp.arange(devices, dtype=jnp.int32)
+    matches = block_order[:, None] == numbers[None, :]
     ordered = jnp.sum(jnp.where(matches, block_rows[None, :], 0), axis=1)
-    before = jnp.cumsum(ordered) - ordered
-    starts = jnp.sum(jnp.where(matches, before[:, None], 0), axis=0)
-    offset = jnp.arange(maxrows, dtype=jnp.int32)
-    in_block = offset[None, :] < block_rows[:, None]
-    target = starts[:, None] + offset[None, :]
-    return (in_block, target)
-
-
-def build_table(block_rows, block_order, ao_to_virt, maxrows):
-    in_block, target = ao_layout(block_rows, block_order, maxrows)
-    row_index = jnp.where(in_block, target, 0).reshape(-1)
-    ao_rows = jnp.take(ao_to_virt, row_index, axis=0)
-    return jnp.where(in_block.reshape(-1, 1), ao_rows, jnp.zeros_like(ao_rows))
-
-
-def contract_rows(ao_table, received):
+    starts = jnp.sum(jnp.where(matches, exclusive_sum(ordered)[:, None], 0), axis=0)
+    offset = jnp.arange(DIRECT, dtype=jnp.int32)
+    direct = jnp.where(offset[None, :] < block_rows[:, None], starts[:, None] + offset[None, :], -1)
+    rest = jnp.maximum(block_rows - DIRECT, 0).reshape(-1, PLANE)
+    first = exclusive_sum(rest)
+    slots = jnp.arange(PLANE * (maxrows - DIRECT), dtype=jnp.int32)
+    inside = (slots >= first[..., None]) & (slots < (first + rest)[..., None])
+    source = (starts.reshape(-1, PLANE) + DIRECT - first)[..., None] + slots
+    packed = jnp.sum(jnp.where(inside, source + 1, 0), axis=1) - 1
+    packed = picked(packed, plane ^ jnp.arange(packed.shape[0], dtype=jnp.int32))
+    targets = jnp.concatenate(
+        [direct.reshape(-1), packed[:, :STEADY].reshape(-1), packed[:, STEADY:].reshape(-1)]
+    )
+    senders = in_plane ^ jnp.arange(PLANE, dtype=jnp.int32)
+    here = jnp.reshape(plane, (1,))
+    first_here, rest_here = picked(picked(first, here)[0], senders), picked(picked(rest, here)[0], senders)
+    row = jnp.arange(maxrows - DIRECT, dtype=jnp.int32)
+    hot = (slots[:, None, None] == first_here[:, None] + row) & (row < rest_here[:, None])
+    packing = hot.reshape(slots.shape[0], -1).astype(jnp.bfloat16)
+    return targets, packing, jnp.max(jnp.sum(rest, axis=1))
+
+
+def table_of(targets, ao_to_virt):
+    functions = jnp.arange(ao_to_virt.shape[0], dtype=jnp.int32)
+    hot = (functions[:, None] == targets[None, :]).astype(jnp.bfloat16)
     return lax.dot_general(
-        ao_table, received, (((0,), (0,)), ((), ())), preferred_element_type=jnp.float32
+        ao_to_virt, hot, (((0,), (0,)), ((), ())), preferred_element_type=jnp.float32
     ).astype(jnp.bfloat16)
 
 
@@ -59,6 +90,96 @@
 
 def grant(mib):
     return pltpu.CompilerParams(vmem_limit_bytes=mib << 20)
+
+
+def pack_kernel(place_ref, packing_ref, *refs):
+    received, outs, rows_ref = refs[:PLANE], refs[PLANE:-1], refs[-1]
+    steady, over_ref = outs[:-1], outs[-1]
+    rows = received[0].shape[1]
+    for step in range(len(steady)):
+        plane = lax.bitwise_xor(place_ref[2], step)
+        for d, ref in enumerate(received):
+            rows_ref[d * rows : (d + 1) * rows, :] = ref[plane]
+        packed = jnp.dot(packing_ref[...], rows_ref[...], preferred_element_type=jnp.float32)
+        packed = packed.astype(rows_ref.dtype)
+        steady[step][...] = packed[:STEADY]
+        over_ref[step] = packed[STEADY:]
+
+
+def packed_rows(place, packing, received):
+    planes, rows, columns = received[0].shape
+    slots = PLANE * rows
+    return pl.pallas_call(
+        pack_kernel,
+        out_shape=[jax.ShapeDtypeStruct((STEADY, columns), jnp.bfloat16)] * planes
+        + [jax.ShapeDtypeStruct((planes, slots - STEADY, columns), jnp.bfloat16)],
+        in_specs=[IN_SMEM] + [IN_VMEM] * (1 + PLANE),
+        out_specs=[IN_VMEM] * (planes + 1),
+        scratch_shapes=[pltpu.VMEM((slots, columns), jnp.bfloat16)],
+        compiler_params=grant(6),
+        cost_estimate=pl.CostEstimate(
+            flops=2 * planes * slots * slots * columns,
+            bytes_accessed=4 * planes * slots * columns,
+            transcendentals=0,
+        ),
+    )(place, packing, *received)
+
+
+def tile_kernel(table_ref, direct_ref, *refs):
+    steady, over_ref, out_ref, rows_ref = refs[:-3], refs[-3], refs[-2], refs[-1]
+    count = direct_ref.shape[0]
+    for step, ref in enumerate(steady):
+        rows_ref[step * STEADY : (step + 1) * STEADY, :] = ref[...]
+    done = len(steady) * STEADY
+    rows_ref[done:, :] = over_ref[...]
+    total = jnp.dot(table_ref[:, :count], direct_ref[...], preferred_element_type=jnp.float32)
+    total += jnp.dot(table_ref[:, count:], rows_ref[...], preferred_element_type=jnp.float32)
+    out_ref[...] = total.astype(out_ref.dtype)
+
+
+def tile_of(table, direct, steady, over):
+    vt, rows = table.shape
+    columns = direct.shape[1]
+    return pl.pallas_call(
+        tile_kernel,
+        out_shape=jax.ShapeDtypeStruct((vt, columns), jnp.bfloat16),
+        in_specs=[IN_VMEM] * (3 + len(steady)),
+        out_specs=IN_VMEM,
+        scratch_shapes=[pltpu.VMEM((rows - direct.shape[0], columns), jnp.bfloat16)],
+        compiler_params=grant(12),
+        cost_estimate=pl.CostEstimate(
+            flops=2 * vt * rows * columns,
+            bytes_accessed=2 * (vt * rows + rows * columns + vt * columns),
+            transcendentals=0,
+        ),
+    )(table, direct, *steady, over)
+
+
+def own_tile_of(half_blocks, block_rows, block_order, ao_to_virt, place, position):
+    maxrows, devices, columns = half_blocks.shape
+    rest = maxrows - DIRECT
+    planes = devices // PLANE
+    plane, in_plane = position // PLANE, position % PLANE
+    direct = sent_to_owners(half_blocks[:DIRECT])
+    targets, packing, most = row_layout(block_rows, block_order, maxrows, plane, in_plane)
+    table = table_of(targets, ao_to_virt)
+    by_owner = jnp.transpose(half_blocks[DIRECT:], (1, 0, 2)).reshape(planes, PLANE, rest, columns)
+    received = []
+    for d in range(PLANE):
+        block = lax.dynamic_index_in_dim(by_owner, in_plane ^ d, 1, keepdims=False)
+        received.append(crossed(block, d) if d else block)
+    *steady, over = packed_rows(place, packing, received)
+    arrived = [steady[0]] + [crossed(steady[m], m * PLANE) for m in range(1, planes)]
+
+    def overflow(rows):
+        return jnp.stack([rows[0]] + [crossed(rows[m], m * PLANE) for m in range(1, planes)])
+
+    over = lax.cond(most > STEADY, overflow, jnp.zeros_like, over)
+    return tile_of(table, direct, arrived, over.reshape(-1, columns))
+
+
+def sent_to_owners(rows):
+    return lax.all_to_all(rows, "occ", split_axis=1, concat_axis=0, tiled=True)[:, 0, :]
 
 
 def pair_kernel(own_ref, *refs):
@@ -113,32 +234,40 @@
     )(blocks)
 
 
-def amplitude_kernel(steps, place_ref, energy_ref, column_ref, row_ref, one_ref, two_ref, out_ref):
+def amplitude_kernel(groups, place_ref, energy_ref, column_ref, row_ref, *refs):
+    parts, out_ref = refs[:-1], refs[-1]
     copies, _, rows, _ = out_ref.shape
     occupied = energy_ref.shape[0]
     position = place_ref[0]
     block = pl.ds(pl.multiple_of(place_ref[1] * rows, rows), rows)
     both = column_ref[block, :] + row_ref[...]
-    for k, step in enumerate(steps):
-        partner = lax.rem(position + occupied - step, occupied)
-        gap = both - energy_ref[position] - energy_ref[partner]
-        merged = one_ref[k].astype(jnp.float32) + two_ref[k].astype(jnp.float32)
-        amplitude = (merged / gap).astype(out_ref.dtype)
-        for copy in range(copies):
-            out_ref[copy, k] = amplitude
-
-
-def amplitude_of(steps, place, energies, column, row, one, two):
-    return pl.pallas_call(
-        functools.partial(amplitude_kernel, steps),
-        out_shape=jax.ShapeDtypeStruct((XS,) + one.shape, jnp.bfloat16),
-        in_specs=[IN_SMEM] * 2 + [IN_VMEM] * 4,
+    done = 0
+    for group, steps in enumerate(groups):
+        one_ref, two_ref = parts[2 * group : 2 * group + 2]
+        for k, step in enumerate(steps):
+            partner = lax.rem(position + occupied - step, occupied)
+            gap = both - energy_ref[position] - energy_ref[partner]
+            merged = one_ref[k].astype(jnp.float32) + two_ref[k].astype(jnp.float32)
+            amplitude = (merged / gap).astype(out_ref.dtype)
+            for copy in range(copies):
+                out_ref[copy, done + k] = amplitude
+        done += len(steps)
+
+
+def amplitude_of(groups, place, energies, column, row, parts):
+    count = sum(len(steps) for steps in groups)
+    shape = (XS, count) + parts[0][0].shape[1:]
+    size = math.prod(shape[1:])
+    return pl.pallas_call(
+        functools.partial(amplitude_kernel, groups),
+        out_shape=jax.ShapeDtypeStruct(shape, jnp.bfloat16),
+        in_specs=[IN_SMEM] * 2 + [IN_VMEM] * (2 + 2 * len(groups)),
         out_specs=IN_VMEM,
         compiler_params=grant(6),
         cost_estimate=pl.CostEstimate(
-            flops=6 * one.size, bytes_accessed=12 * one.size, transcendentals=0
-        ),
-    )(place, energies, column, row, one, two)
+            flops=6 * size, bytes_accessed=12 * size, transcendentals=0
+        ),
+    )(place, energies, column, row, *[array for pair in parts for array in pair])
 
 
 def density_kernel(counts, *refs):
@@ -181,29 +310,30 @@
 
 
 GROUPS = ((0,), (1, 2), (3,))
+HALVES = ((0, 2), (2, 3))
 
 
 def shards(half_blocks, block_rows, block_order, ao_to_virt, occ_energy, virt_energy):
-    maxrows = half_blocks.shape[0]
-    place = jnp.stack([lax.axis_index("occ"), lax.axis_index("aux") // ZS]).astype(jnp.int32)
+    position = lax.axis_index("occ").astype(jnp.int32)
+    place = jnp.stack(
+        [position, lax.axis_index("aux").astype(jnp.int32) // ZS, position // PLANE]
+    )
     column, row = virt_energy[:, None], virt_energy[None, :]
-    ao_table = build_table(block_rows, block_order, ao_to_virt, maxrows)
-    own_tile = contract_rows(
-        ao_table,
-        lax.all_to_all(half_blocks, "occ", split_axis=1, concat_axis=0, tiled=True)[:, 0, :],
-    )
+    own_tile = own_tile_of(half_blocks, block_rows, block_order, ao_to_virt, place, position)
     tiles = [own_tile, shifted(own_tile, "occ", 1), shifted(own_tile, "occ", 2)]
     tiles.append(shifted(tiles[2], "occ", 1))
-    amplitudes = []
+    parts = []
     for steps in GROUPS:
         blocks = pair_blocks(own_tile, [tiles[k] for k in steps])
-        received = exchanged_x(blocks)
-        part = sum_of(received)
-        other = swapped_z(part)
-        amplitude = amplitude_of(steps, place, occ_energy, column, row, part, other)
-        amplitudes.append(exchanged_x(amplitude))
-    density = density_of(amplitudes[:2], tiles[:3])
-    return density_of(amplitudes[2:], tiles[3:], density)[None]
+        part = sum_of(exchanged_x(blocks))
+        parts.append((part, swapped_z(part)))
+    density = None
+    for lo, hi in HALVES:
+        amplitude = amplitude_of(GROUPS[lo:hi], place, occ_energy, column, row, parts[lo:hi])
+        amplitude = exchanged_x(amplitude)
+        steps = [k for group in GROUPS[lo:hi] for k in group]
+        density = density_of([amplitude], [tiles[k] for k in steps], density)
+    return density[None]
 
 
 def solution(mesh):

time: 286 us -> 284 us (level)
  the two profiles are of different devices: /device:TPU:1 before, /device:TPU:56 now
where the time goes in v2:
time: 284 us; the launch traced here: 282 us
  starting transfers between devices  121 us (43%)
  waiting for transfers between devices  103 us (36%)
  Pallas kernels  26.5 us (9%)
  local copies, waits for them, and re-layouts  23.5 us (8%)
  other arithmetic  4.58 us (2%)
    ppermute x14, starting transfers between devices, crossed(): return lax.ppermute(value, 'occ', [(i, i ^ mask) for i in range(devices)])  51.9 us
    ppermute x3, waiting for transfers between devices, swapped_z(): return lax.ppermute(value, 'aux', perm)  39.5 us
    ppermute x14, waiting for transfers between devices, crossed(): return lax.ppermute(value, 'occ', [(i, i ^ mask) for i in range(devices)])  31.2 us
    ppermute x3, starting transfers between devices, swapped_z(): return lax.ppermute(value, 'aux', perm)  22.8 us
    all_to_all x5, starting transfers between devices, exchanged_x(): lax.all_to_all(value, 'aux', 0, 0, axis_index_groups=groups, tiled=True)  21.4 us
    all_to_all x5, waiting for transfers between devices, exchanged_x(): lax.all_to_all(value, 'aux', 0, 0, axis_index_groups=groups, tiled=True)  18.8 us
    unnamed x41, local copies, waits for them, and re-layouts  15.8 us
    all_to_all x1, starting transfers between devices, sent_to_owners(): lax.all_to_all(rows, 'occ', split_axis=1, concat_axis=0, tiled=True)  15.4 us
  transfers between devices with their start and end apart: 26, of which 10 were waited for; matrix products, arithmetic and copies ran while one was open for 6% of the time, Pallas kernels for 7%

profile of v2, /device:TPU:56, one launch (start us, length us, event | category | flops | bytes accessed | tf_op | source)
XLA Modules:
  0.0 282.1 jit_solution(4507638163647171204)
XLA Ops:
  1.6 4.1 %constant_dynamic-slice_fusion = (bf16[8,1,16,768]{3,1,0,2:T(2,128)(2,1)S(1)}, bf16[8,1,16,768]{3,1,0,2:T(2,128)(2,1)S(1)}, bf16[8,1,16,768]{3,1,0,2:T(2,128)(2,...) fusion(bf16[8,8,16,768]{3,1,0,2:T(8,128)(2,1)S(1)} %slice_bitca, ...), kind=kLoop, calls=%fused_computation.55 | loop fusion | bytes 3145760 | tf_op jit(solution)/shard_map/jit(dynamic_index_in_dim)/dynamic_slice | solution.py:169
  6.6 3.1 %collective-permute-start.10 = (bf16[8,16,768]{2,1,0:T(8,128)(2,1)}, bf16[8,16,768]{2,1,0:T(8,128)(2,1)S(1)}, u32[]{:S(2)}, u32[]{:S(2)}) collective-permute-start(bf16[8,16,768]{2,1,0:T(8,128)(2,1)} %bitcast.74), channel_id=1, source_target_pairs={{0,32},{8,40},{16,48},{24,56},{32,0},{40,8},{48,16},{56,24},{64,96... | collective-permute-start | bytes 589832 | tf_op jit(solution)/shard_map/ppermute | solution.py:36
  10.5 3.4 %collective-permute-start.11 = (bf16[8,16,768]{2,1,0:T(8,128)(2,1)}, bf16[8,16,768]{2,1,0:T(8,128)(2,1)S(1)}, u32[]{:S(2)}, u32[]{:S(2)}) collective-permute-start(bf16[8,16,768]{2,1,0:T(8,128)(2,1)} %bitcast.73), channel_id=1, source_target_pairs={{0,40},{8,32},{16,56},{24,48},{32,8},{40,0},{48,24},{56,16},{64,10... | collective-permute-start | bytes 589832 | tf_op jit(solution)/shard_map/ppermute | solution.py:36
  18.1 4.7 %collective-permute-start.13 = (bf16[8,16,768]{2,1,0:T(8,128)(2,1)}, bf16[8,16,768]{2,1,0:T(8,128)(2,1)S(1)}, u32[]{:S(2)}, u32[]{:S(2)}) collective-permute-start(bf16[8,16,768]{2,1,0:T(8,128)(2,1)} %bitcast.71), channel_id=1, source_target_pairs={{0,56},{8,48},{16,40},{24,32},{32,24},{40,16},{48,8},{56,0},{64,12... | collective-permute-start | bytes 589832 | tf_op jit(solution)/shard_map/ppermute | solution.py:36
  26.9 15.4 %all-to-all-start = ((bf16[8,64,768]{2,0,1:T(8,128)(2,1)}), bf16[8,64,768]{2,0,1:T(8,128)(2,1)S(1)}, u32[]{:S(2)}, u32[]{:S(2)}) async-start(bf16[8,64,768]{2,0,1:T(8,128)(2,1)} %copy.55), calls=%async_computation | async-start | bytes 1572864 | tf_op jit(solution)/shard_map/all_to_all | solution.py:182
  50.8 2.8 collective-permute-start.8
  56.2 5.5 %collective-permute-done.8.refs_2_ = bf16[8,16,768]{2,1,0:T(8,128)(2,1)S(1)} collective-permute-done((bf16[8,16,768]{2,1,0:T(8,128)(2,1)}, bf16[8,16,768]{2,1,0:T(8,128)(2,1)S(1)}, u32[]{:S(2)}, u32[]{:S(2)}) %collective-permute-start.8) | collective-permute-done | bytes 196640 | tf_op jit(solution)/shard_map/ppermute | solution.py:36
  61.7 3.9 %collective-permute-done.9.refs_3_ = bf16[8,16,768]{2,1,0:T(8,128)(2,1)S(1)} collective-permute-done((bf16[8,16,768]{2,1,0:T(8,128)(2,1)}, bf16[8,16,768]{2,1,0:T(8,128)(2,1)S(1)}, u32[]{:S(2)}, u32[]{:S(2)}) %collective-permute-start.9) | collective-permute-done | bytes 196640 | tf_op jit(solution)/shard_map/ppermute | solution.py:36
  71.2 5.6 %collective-permute-start.15 = (bf16[80,768]{1,0:T(8,128)(2,1)S(1)}, bf16[80,768]{1,0:T(8,128)(2,1)S(1)}, u32[]{:S(2)}, u32[]{:S(2)}) collective-permute-start(bf16[80,768]{1,0:T(8,128)(2,1)S(1)} %get-tuple-element.21), channel_id=1, source_target_pairs={{0,128},{8,136},{16,144},{24,152},{32,160},{40,168},{48,176},{56,1... | collective-permute-start | bytes 368648 | tf_op jit(solution)/shard_map/ppermute | solution.py:36
  79.2 7.3 %collective-permute-start.17 = (bf16[80,768]{1,0:T(8,128)(2,1)S(1)}, bf16[80,768]{1,0:T(8,128)(2,1)S(1)}, u32[]{:S(2)}, u32[]{:S(2)}) collective-permute-start(bf16[80,768]{1,0:T(8,128)(2,1)S(1)} %get-tuple-element.23), channel_id=1, source_target_pairs={{0,256},{8,264},{16,272},{24,280},{32,288},{40,296},{48,304},{56,3... | collective-permute-start | bytes 368648 | tf_op jit(solution)/shard_map/ppermute | solution.py:36
  89.0 8.6 %collective-permute-start.19 = (bf16[80,768]{1,0:T(8,128)(2,1)S(1)}, bf16[80,768]{1,0:T(8,128)(2,1)S(1)}, u32[]{:S(2)}, u32[]{:S(2)}) collective-permute-start(bf16[80,768]{1,0:T(8,128)(2,1)S(1)} %get-tuple-element.25), channel_id=1, source_target_pairs={{0,384},{8,392},{16,400},{24,408},{32,416},{40,424},{48,432},{56,4... | collective-permute-start | bytes 368648 | tf_op jit(solution)/shard_map/ppermute | solution.py:36
  97.6 2.9 %collective-permute-start.20 = (bf16[80,768]{1,0:T(8,128)(2,1)S(1)}, bf16[80,768]{1,0:T(8,128)(2,1)S(1)}, u32[]{:S(2)}, u32[]{:S(2)}) collective-permute-start(bf16[80,768]{1,0:T(8,128)(2,1)S(1)} %get-tuple-element.26), channel_id=1, source_target_pairs={{0,448},{8,456},{16,464},{24,472},{32,480},{40,488},{48,496},{56,5... | collective-permute-start | bytes 368648 | tf_op jit(solution)/shard_map/ppermute | solution.py:36
  103.2 21.8 %collective-permute-done.18.refs_5_ = bf16[80,768]{1,0:T(8,128)(2,1)S(1)} collective-permute-done((bf16[80,768]{1,0:T(8,128)(2,1)S(1)}, bf16[80,768]{1,0:T(8,128)(2,1)S(1)}, u32[]{:S(2)}, u32[]{:S(2)}) %collective-permute-start.18) | collective-permute-done | bytes 122912 | tf_op jit(solution)/shard_map/ppermute | solution.py:36
  128.9 5.4 %collective-permute-start.21 = (bf16[512,768]{1,0:T(8,128)(2,1)S(1)}, bf16[512,768]{1,0:T(8,128)(2,1)}, u32[]{:S(2)}, u32[]{:S(2)}) collective-permute-start(bf16[512,768]{1,0:T(8,128)(2,1)S(1)} %shard_map.65.own_ref.refs_0_.refs_1_), channel_id=1, source_target_pairs={{0,16},{8,24},{16,32},{24,40},{32,48},{40,56},{48,64},{56,72},{64,... | collective-permute-start | bytes 2359304 | tf_op jit(solution)/shard_map/ppermute | solution.py:21
  139.2 4.3 %all-to-all-start.3 = ((bf16[4,1,128,512]{3,2,1,0:T(8,128)(2,1)}), bf16[4,1,128,512]{3,2,1,0:T(8,128)(2,1)S(1)}, u32[]{:S(2)}, u32[]{:S(2)}) async-start(bf16[4,1,128,512]{3,2,1,0:T(8,128)(2,1)} %copy-done.8), calls=%async_computation.3 | async-start | bytes 1048576 | tf_op jit(solution)/shard_map/all_to_all | solution.py:26
  143.6 8.7 %collective-permute-done.21.refs_1_.refs_3_ = bf16[512,768]{1,0:T(8,128)(2,1)} collective-permute-done((bf16[512,768]{1,0:T(8,128)(2,1)S(1)}, bf16[512,768]{1,0:T(8,128)(2,1)}, u32[]{:S(2)}, u32[]{:S(2)}) %collective-permute-start.21) | collective-permute-done | bytes 786464 | tf_op jit(solution)/shard_map/ppermute | solution.py:21
  154.4 4.4 %collective-permute-done.25.refs_0_.refs_2_ = bf16[512,768]{1,0:T(8,128)(2,1)S(1)} collective-permute-done((bf16[512,768]{1,0:T(8,128)(2,1)S(1)}, bf16[512,768]{1,0:T(8,128)(2,1)S(1)}, u32[]{:S(2)}, u32[]{:S(2)}) %collective-permute-start.25) | collective-permute-done | bytes 786464 | tf_op jit(solution)/shard_map/ppermute | solution.py:21
  158.8 5.6 %shard_map.71 = bf16[4,2,128,512]{3,2,1,0:T(8,128)(2,1)S(1)} custom-call(bf16[512,768]{1,0:T(8,128)(2,1)S(1)} %shard_map.65.own_ref.refs_0_.refs_1_, bf16[512,768]{1,0:T(8,128)(2,1)S(1)} %collective-permute-done.25.refs_0_.refs_2_, bf16[512,768]{1,0:T(8,128)(2,1)} %collective-permute-done.21.refs_1_.refs_3_), custom_call_target="tpu_custom_call" | custom-call | flops 1610612736 | bytes 3407872 | tf_op jit(solution)/shard_map/pallas_call | solution.py:203
  165.4 4.3 %all-to-all-start.4 = ((bf16[4,2,128,512]{3,2,1,0:T(8,128)(2,1)}), bf16[4,2,128,512]{3,2,1,0:T(8,128)(2,1)S(1)}, u32[]{:S(2)}, u32[]{:S(2)}) async-start(bf16[4,2,128,512]{3,2,1,0:T(8,128)(2,1)} %copy-done.4), calls=%async_computation.4 | async-start | bytes 2097152 | tf_op jit(solution)/shard_map/all_to_all | solution.py:26
  169.7 3.3 %shard_map.66 = bf16[4,1,128,512]{3,2,1,0:T(8,128)(2,1)S(1)} custom-call(bf16[512,768]{1,0:T(8,128)(2,1)S(1)} %shard_map.65.own_ref.refs_0_.refs_1_, bf16[512,768]{1,0:T(8,128)(2,1)} %collective-permute-done.22.refs_0_.refs_1_), custom_call_target="tpu_custom_call" | custom-call | flops 805306368 | bytes 2097152 | tf_op jit(solution)/shard_map/pallas_call | solution.py:203
  173.8 12.3 %all-to-all-done.4.blocks_ref = bf16[4,2,128,512]{3,2,1,0:T(8,128)(2,1)S(1)} async-done(((bf16[4,2,128,512]{3,2,1,0:T(8,128)(2,1)}), bf16[4,2,128,512]{3,2,1,0:T(8,128)(2,1)S(1)}, u32[]{:S(2)}, u32[]{:S(2)}) %all-to-all-start.4) | async-done | bytes 1048608 | tf_op jit(solution)/shard_map/all_to_all | solution.py:26
  186.1 4.1 %all-to-all-start.1 = ((bf16[4,1,128,512]{3,2,1,0:T(8,128)(2,1)}), bf16[4,1,128,512]{3,2,1,0:T(8,128)(2,1)}, u32[]{:S(2)}, u32[]{:S(2)}) async-start(bf16[4,1,128,512]{3,2,1,0:T(8,128)(2,1)} %copy-done.7), calls=%async_computation.1 | async-start | bytes 1048576 | tf_op jit(solution)/shard_map/all_to_all | solution.py:26
  191.1 8.2 %collective-permute-start.26 = (bf16[2,128,512]{2,1,0:T(8,128)(2,1)}, bf16[2,128,512]{2,1,0:T(8,128)(2,1)S(1)}, u32[]{:S(2)}, u32[]{:S(2)}) collective-permute-start(bf16[2,128,512]{2,1,0:T(8,128)(2,1)} %shard_map.72.refs_2_), channel_id=1, source_target_pairs={{0,1},{1,0},{2,3},{3,2},{4,5},{5,4},{6,7},{7,6},{8,9},{9,8},{10,11... | collective-permute-start | bytes 786440 | tf_op jit(solution)/shard_map/ppermute | solution.py:31
  199.3 6.4 %collective-permute-start.24 = (bf16[1,128,512]{2,1,0:T(8,128)(2,1)S(1)}, bf16[1,128,512]{2,1,0:T(8,128)(2,1)S(1)}, u32[]{:S(2)}, u32[]{:S(2)}) collective-permute-start(bf16[1,128,512]{2,1,0:T(8,128)(2,1)S(1)} %shard_map.70.refs_0_), channel_id=1, source_target_pairs={{0,1},{1,0},{2,3},{3,2},{4,5},{5,4},{6,7},{7,6},{8,9},{9,8},{10,11... | collective-permute-start | bytes 393224 | tf_op jit(solution)/shard_map/ppermute | solution.py:31
  205.9 32.2 %collective-permute-done.24.refs_1_ = bf16[1,128,512]{2,1,0:T(8,128)(2,1)S(1)} collective-permute-done((bf16[1,128,512]{2,1,0:T(8,128)(2,1)S(1)}, bf16[1,128,512]{2,1,0:T(8,128)(2,1)S(1)}, u32[]{:S(2)}, u32[]{:S(2)}) %collective-permute-start.24) | collective-permute-done | bytes 131104 | tf_op jit(solution)/shard_map/ppermute | solution.py:31
  240.4 4.6 %all-to-all-start.5 = ((bf16[4,3,128,512]{3,2,1,0:T(8,128)(2,1)}), bf16[4,3,128,512]{3,2,1,0:T(8,128)(2,1)S(1)}, u32[]{:S(2)}, u32[]{:S(2)}) async-start(bf16[4,3,128,512]{3,2,1,0:T(8,128)(2,1)} %copy-done.1), calls=%async_computation.5 | async-start | bytes 3145728 | tf_op jit(solution)/shard_map/all_to_all | solution.py:26
  246.1 8.3 %collective-permute-start.23 = (bf16[1,128,512]{2,1,0:T(8,128)(2,1)S(1)}, bf16[1,128,512]{2,1,0:T(8,128)(2,1)S(1)}, u32[]{:S(2)}, u32[]{:S(2)}) collective-permute-start(bf16[1,128,512]{2,1,0:T(8,128)(2,1)S(1)} %shard_map.67.refs_0_), channel_id=1, source_target_pairs={{0,1},{1,0},{2,3},{3,2},{4,5},{5,4},{6,7},{7,6},{8,9},{9,8},{10,11... | collective-permute-start | bytes 393224 | tf_op jit(solution)/shard_map/ppermute | solution.py:31
  254.4 7.3 %collective-permute-done.23.refs_1_ = bf16[1,128,512]{2,1,0:T(8,128)(2,1)S(1)} collective-permute-done((bf16[1,128,512]{2,1,0:T(8,128)(2,1)S(1)}, bf16[1,128,512]{2,1,0:T(8,128)(2,1)S(1)}, u32[]{:S(2)}, u32[]{:S(2)}) %collective-permute-start.23) | collective-permute-done | bytes 131104 | tf_op jit(solution)/shard_map/ppermute | solution.py:31
  265.7 4.1 %all-to-all-start.2 = ((bf16[4,1,128,512]{3,2,1,0:T(8,128)(2,1)}), bf16[4,1,128,512]{3,2,1,0:T(8,128)(2,1)}, u32[]{:S(2)}, u32[]{:S(2)}) async-start(bf16[4,1,128,512]{3,2,1,0:T(8,128)(2,1)} %copy-done.2), calls=%async_computation.2 | async-start | bytes 1048576 | tf_op jit(solution)/shard_map/all_to_all | solution.py:26
  271.0 3.7 %shard_map.74.refs_2_ = f32[512,768]{1,0:T(8,128)} custom-call(bf16[4,3,128,512]{3,2,1,0:T(8,128)(2,1)S(1)} %all-to-all-done.5.refs_0_, bf16[512,768]{1,0:T(8,128)(2,1)S(1)} %shard_map.65.own_ref.refs_0_.refs_1_, bf16[512,768]{1,0:T(8,128)(2,1)S(1)} %copy-done.6, bf16[512,768]{1,0:T(8,128)(2,1)} %collective-permute-done.21.refs_1_.refs_3_), custom_call_target="tpu_custom_call" | custom-call | flops 1207959552 | bytes 5505024 | tf_op jit(solution)/shard_map/pallas_call | solution.py:297
  274.6 3.9 %all-to-all-done.2.refs_0_ = bf16[4,1,128,512]{3,2,1,0:T(8,128)(2,1)} async-done(((bf16[4,1,128,512]{3,2,1,0:T(8,128)(2,1)}), bf16[4,1,128,512]{3,2,1,0:T(8,128)(2,1)}, u32[]{:S(2)}, u32[]{:S(2)}) %all-to-all-start.2) | async-done | bytes 524320 | tf_op jit(solution)/shard_map/all_to_all | solution.py:26
  278.6 3.5 %shard_map.75 = f32[512,768]{1,0:T(8,128)} custom-call(bf16[4,1,128,512]{3,2,1,0:T(8,128)(2,1)} %all-to-all-done.2.refs_0_, bf16[512,768]{1,0:T(8,128)(2,1)} %collective-permute-done.22.refs_0_.refs_1_, f32[512,768]{1,0:T(8,128)} %shard_map.74.refs_2_), custom_call_target="tpu_custom_call", output_to_operand_aliasing={{}: (2, {})} | custom-call | flops 402653184 | bytes 2883584 | tf_op jit(solution)/shard_map/pallas_call | solution.py:297
  (118 shorter events, 58.0 us)
Async XLA Ops:
  0.0 100.6 %copy-start = (bf16[768,512]{1,0:T(8,128)(2,1)S(1)}, bf16[768,512]{1,0:T(8,128)(2,1)}, u32[]{:S(2)}) copy-start(bf16[768,512]{1,0:T(8,128)(2,1)} %param.11) | copy-start | bytes 2359300
  6.6 44.2 %collective-permute-start.10 = (bf16[8,16,768]{2,1,0:T(8,128)(2,1)}, bf16[8,16,768]{2,1,0:T(8,128)(2,1)S(1)}, u32[]{:S(2)}, u32[]{:S(2)}) collective-permute-start(bf16[8,16,768]{2,1,0:T(8,128)(2,1)} %bitcast.74), channel_id=1, source_target_pairs={{0,32},{8,40},{16,48},{24,56},{32,0},{40,8},{48,16},{56,24},{64,96... | collective-permute-start | bytes 589832 | tf_op jit(solution)/shard_map/ppermute | solution.py:36
  10.5 43.1 %collective-permute-start.11 = (bf16[8,16,768]{2,1,0:T(8,128)(2,1)}, bf16[8,16,768]{2,1,0:T(8,128)(2,1)S(1)}, u32[]{:S(2)}, u32[]{:S(2)}) collective-permute-start(bf16[8,16,768]{2,1,0:T(8,128)(2,1)} %bitcast.73), channel_id=1, source_target_pairs={{0,40},{8,32},{16,56},{24,48},{32,8},{40,0},{48,24},{56,16},{64,10... | collective-permute-start | bytes 589832 | tf_op jit(solution)/shard_map/ppermute | solution.py:36
  13.9 11.7 %slice-start = ((bf16[24,64,768]{2,1,0:T(8,128)(2,1)}), bf16[8,64,768]{2,1,0:T(8,128)(2,1)S(1)}, s32[]{:S(2)}) async-start(bf16[24,64,768]{2,1,0:T(8,128)(2,1)} %param.8), calls=%async_computation.6 | async-start | bytes 1572864 | tf_op jit(solution)/shard_map/slice | solution.py:163
  14.7 41.5 %collective-permute-start.12 = (bf16[8,16,768]{2,1,0:T(8,128)(2,1)}, bf16[8,16,768]{2,1,0:T(8,128)(2,1)S(1)}, u32[]{:S(2)}, u32[]{:S(2)}) collective-permute-start(bf16[8,16,768]{2,1,0:T(8,128)(2,1)} %bitcast.72), channel_id=1, source_target_pairs={{0,48},{8,56},{16,32},{24,40},{32,16},{40,24},{48,0},{56,8},{64,11... | collective-permute-start | bytes 589832 | tf_op jit(solution)/shard_map/ppermute | solution.py:36
  18.1 38.1 %collective-permute-start.13 = (bf16[8,16,768]{2,1,0:T(8,128)(2,1)}, bf16[8,16,768]{2,1,0:T(8,128)(2,1)S(1)}, u32[]{:S(2)}, u32[]{:S(2)}) collective-permute-start(bf16[8,16,768]{2,1,0:T(8,128)(2,1)} %bitcast.71), channel_id=1, source_target_pairs={{0,56},{8,48},{16,40},{24,32},{32,24},{40,16},{48,8},{56,0},{64,12... | collective-permute-start | bytes 589832 | tf_op jit(solution)/shard_map/ppermute | solution.py:36
  23.6 32.6 %collective-permute-start.7 = (bf16[8,16,768]{2,1,0:T(8,128)(2,1)}, bf16[8,16,768]{2,1,0:T(8,128)(2,1)S(1)}, u32[]{:S(2)}, u32[]{:S(2)}) collective-permute-start(bf16[8,16,768]{2,1,0:T(8,128)(2,1)} %bitcast.77), channel_id=1, source_target_pairs={{0,8},{8,0},{16,24},{24,16},{32,40},{40,32},{48,56},{56,48},{64,72... | collective-permute-start | bytes 589832 | tf_op jit(solution)/shard_map/ppermute | solution.py:36
  25.5 16.8 %copy-start.14 = (s32[64]{0:T(128)S(1)}, s32[64]{0:T(128)}, u32[]{:S(2)}) copy-start(s32[64]{0:T(128)} %param.9) | copy-start | bytes 772
  26.9 98.2 %all-to-all-start = ((bf16[8,64,768]{2,0,1:T(8,128)(2,1)}), bf16[8,64,768]{2,0,1:T(8,128)(2,1)S(1)}, u32[]{:S(2)}, u32[]{:S(2)}) async-start(bf16[8,64,768]{2,0,1:T(8,128)(2,1)} %copy.55), calls=%async_computation | async-start | bytes 1572864 | tf_op jit(solution)/shard_map/all_to_all | solution.py:182
  50.8 10.9 %collective-permute-start.8 = (bf16[8,16,768]{2,1,0:T(8,128)(2,1)}, bf16[8,16,768]{2,1,0:T(8,128)(2,1)S(1)}, u32[]{:S(2)}, u32[]{:S(2)}) collective-permute-start(bf16[8,16,768]{2,1,0:T(8,128)(2,1)} %bitcast.86), channel_id=1, source_target_pairs={{0,16},{8,24},{16,0},{24,8},{32,48},{40,56},{48,32},{56,40},{64,80... | collective-permute-start | bytes 589832 | tf_op jit(solution)/shard_map/ppermute | solution.py:36
  53.6 12.0 %collective-permute-start.9 = (bf16[8,16,768]{2,1,0:T(8,128)(2,1)}, bf16[8,16,768]{2,1,0:T(8,128)(2,1)S(1)}, u32[]{:S(2)}, u32[]{:S(2)}) collective-permute-start(bf16[8,16,768]{2,1,0:T(8,128)(2,1)} %bitcast.85), channel_id=1, source_target_pairs={{0,24},{8,16},{16,8},{24,0},{32,56},{40,48},{48,40},{56,32},{64,88... | collective-permute-start | bytes 589832 | tf_op jit(solution)/shard_map/ppermute | solution.py:36
  68.2 9.0 %copy-start.13 = (s32[64,8]{1,0:T(8,128)S(1)}, s32[64,8]{1,0:T(8,128)}, u32[]{:S(2)}) copy-start(s32[64,8]{1,0:T(8,128)} %add_select_fusion) | copy-start | bytes 6148
  69.1 19.9 %collective-permute-start.14 = (bf16[80,768]{1,0:T(8,128)(2,1)S(1)}, bf16[80,768]{1,0:T(8,128)(2,1)S(1)}, u32[]{:S(2)}, u32[]{:S(2)}) collective-permute-start(bf16[80,768]{1,0:T(8,128)(2,1)S(1)} %copy-done.12), channel_id=1, source_target_pairs={{0,64},{8,72},{16,80},{24,88},{32,96},{40,104},{48,112},{56,120},{... | collective-permute-start | bytes 368648 | tf_op jit(solution)/shard_map/ppermute | solution.py:36
  71.2 26.4 %collective-permute-start.15 = (bf16[80,768]{1,0:T(8,128)(2,1)S(1)}, bf16[80,768]{1,0:T(8,128)(2,1)S(1)}, u32[]{:S(2)}, u32[]{:S(2)}) collective-permute-start(bf16[80,768]{1,0:T(8,128)(2,1)S(1)} %get-tuple-element.21), channel_id=1, source_target_pairs={{0,128},{8,136},{16,144},{24,152},{32,160},{40,168},{48,176},{56,1... | collective-permute-start | bytes 368648 | tf_op jit(solution)/shard_map/ppermute | solution.py:36
  77.3 25.9 %collective-permute-start.16 = (bf16[80,768]{1,0:T(8,128)(2,1)}, bf16[80,768]{1,0:T(8,128)(2,1)S(1)}, u32[]{:S(2)}, u32[]{:S(2)}) collective-permute-start(bf16[80,768]{1,0:T(8,128)(2,1)} %get-tuple-element.22), channel_id=1, source_target_pairs={{0,192},{8,200},{16,208},{24,216},{32,224},{40,232},{48,240},{56,2... | collective-permute-start | bytes 368648 | tf_op jit(solution)/shard_map/ppermute | solution.py:36
  79.2 24.0 %collective-permute-start.17 = (bf16[80,768]{1,0:T(8,128)(2,1)S(1)}, bf16[80,768]{1,0:T(8,128)(2,1)S(1)}, u32[]{:S(2)}, u32[]{:S(2)}) collective-permute-start(bf16[80,768]{1,0:T(8,128)(2,1)S(1)} %get-tuple-element.23), channel_id=1, source_target_pairs={{0,256},{8,264},{16,272},{24,280},{32,288},{40,296},{48,304},{56,3... | collective-permute-start | bytes 368648 | tf_op jit(solution)/shard_map/ppermute | solution.py:36
  86.6 38.5 %collective-permute-start.18 = (bf16[80,768]{1,0:T(8,128)(2,1)S(1)}, bf16[80,768]{1,0:T(8,128)(2,1)S(1)}, u32[]{:S(2)}, u32[]{:S(2)}) collective-permute-start(bf16[80,768]{1,0:T(8,128)(2,1)S(1)} %get-tuple-element.24), channel_id=1, source_target_pairs={{0,320},{8,328},{16,336},{24,344},{32,352},{40,360},{48,368},{56,3... | collective-permute-start | bytes 368648 | tf_op jit(solution)/shard_map/ppermute | solution.py:36
  89.0 36.1 %collective-permute-start.19 = (bf16[80,768]{1,0:T(8,128)(2,1)S(1)}, bf16[80,768]{1,0:T(8,128)(2,1)S(1)}, u32[]{:S(2)}, u32[]{:S(2)}) collective-permute-start(bf16[80,768]{1,0:T(8,128)(2,1)S(1)} %get-tuple-element.25), channel_id=1, source_target_pairs={{0,384},{8,392},{16,400},{24,408},{32,416},{40,424},{48,432},{56,4... | collective-permute-start | bytes 368648 | tf_op jit(solution)/shard_map/ppermute | solution.py:36
  97.6 27.4 %collective-permute-start.20 = (bf16[80,768]{1,0:T(8,128)(2,1)S(1)}, bf16[80,768]{1,0:T(8,128)(2,1)S(1)}, u32[]{:S(2)}, u32[]{:S(2)}) collective-permute-start(bf16[80,768]{1,0:T(8,128)(2,1)S(1)} %get-tuple-element.26), channel_id=1, source_target_pairs={{0,448},{8,456},{16,464},{24,472},{32,480},{40,488},{48,496},{56,5... | collective-permute-start | bytes 368648 | tf_op jit(solution)/shard_map/ppermute | solution.py:36
  128.9 23.3 %collective-permute-start.21 = (bf16[512,768]{1,0:T(8,128)(2,1)S(1)}, bf16[512,768]{1,0:T(8,128)(2,1)}, u32[]{:S(2)}, u32[]{:S(2)}) collective-permute-start(bf16[512,768]{1,0:T(8,128)(2,1)S(1)} %shard_map.65.own_ref.refs_0_.refs_1_), channel_id=1, source_target_pairs={{0,16},{8,24},{16,32},{24,40},{32,48},{40,56},{48,64},{56,72},{64,... | collective-permute-start | bytes 2359304 | tf_op jit(solution)/shard_map/ppermute | solution.py:21
  134.4 24.4 %collective-permute-start.25 = (bf16[512,768]{1,0:T(8,128)(2,1)S(1)}, bf16[512,768]{1,0:T(8,128)(2,1)S(1)}, u32[]{:S(2)}, u32[]{:S(2)}) collective-permute-start(bf16[512,768]{1,0:T(8,128)(2,1)S(1)} %shard_map.65.own_ref.refs_0_.refs_1_), channel_id=1, source_target_pairs={{0,8},{8,16},{16,24},{24,32},{32,40},{40,48},{48,56},{56,64},{64,7... | collective-permute-start | bytes 2359304 | tf_op jit(solution)/shard_map/ppermute | solution.py:21
  139.2 26.1 %all-to-all-start.3 = ((bf16[4,1,128,512]{3,2,1,0:T(8,128)(2,1)}), bf16[4,1,128,512]{3,2,1,0:T(8,128)(2,1)S(1)}, u32[]{:S(2)}, u32[]{:S(2)}) async-start(bf16[4,1,128,512]{3,2,1,0:T(8,128)(2,1)} %copy-done.8), calls=%async_computation.3 | async-start | bytes 1048576 | tf_op jit(solution)/shard_map/all_to_all | solution.py:26
  152.3 17.4 %collective-permute-start.22 = (bf16[512,768]{1,0:T(8,128)(2,1)}, bf16[512,768]{1,0:T(8,128)(2,1)}, u32[]{:S(2)}, u32[]{:S(2)}) collective-permute-start(bf16[512,768]{1,0:T(8,128)(2,1)} %collective-permute-done.21.refs_1_.refs_3_), channel_id=1, source_target_pairs={{0,8},{8,16},{16,24},{24,32},{32,40},{40,48},{48,56},{56,64},{64,7... | collective-permute-start | bytes 2359304 | tf_op jit(solution)/shard_map/ppermute | solution.py:21
  165.4 20.7 %all-to-all-start.4 = ((bf16[4,2,128,512]{3,2,1,0:T(8,128)(2,1)}), bf16[4,2,128,512]{3,2,1,0:T(8,128)(2,1)S(1)}, u32[]{:S(2)}, u32[]{:S(2)}) async-start(bf16[4,2,128,512]{3,2,1,0:T(8,128)(2,1)} %copy-done.4), calls=%async_computation.4 | async-start | bytes 2097152 | tf_op jit(solution)/shard_map/all_to_all | solution.py:26
  173.8 31.9 %copy-start.9 = (f32[512]{0:T(512)S(1)}, f32[512]{0:T(512)}, u32[]{:S(2)}) copy-start(f32[512]{0:T(512)} %param.13) | copy-start | bytes 6148
  173.8 64.2 %copy-start.10 = (f32[64]{0:T(128)S(1)}, f32[64]{0:T(128)}, u32[]{:S(2)}) copy-start(f32[64]{0:T(128)} %energy_ref.3) | copy-start | bytes 772
  186.1 54.3 %all-to-all-start.1 = ((bf16[4,1,128,512]{3,2,1,0:T(8,128)(2,1)}), bf16[4,1,128,512]{3,2,1,0:T(8,128)(2,1)}, u32[]{:S(2)}, u32[]{:S(2)}) async-start(bf16[4,1,128,512]{3,2,1,0:T(8,128)(2,1)} %copy-done.7), calls=%async_computation.1 | async-start | bytes 1048576 | tf_op jit(solution)/shard_map/all_to_all | solution.py:26
  191.1 47.0 %collective-permute-start.26 = (bf16[2,128,512]{2,1,0:T(8,128)(2,1)}, bf16[2,128,512]{2,1,0:T(8,128)(2,1)S(1)}, u32[]{:S(2)}, u32[]{:S(2)}) collective-permute-start(bf16[2,128,512]{2,1,0:T(8,128)(2,1)} %shard_map.72.refs_2_), channel_id=1, source_target_pairs={{0,1},{1,0},{2,3},{3,2},{4,5},{5,4},{6,7},{7,6},{8,9},{9,8},{10,11... | collective-permute-start | bytes 786440 | tf_op jit(solution)/shard_map/ppermute | solution.py:31
  199.3 38.7 %collective-permute-start.24 = (bf16[1,128,512]{2,1,0:T(8,128)(2,1)S(1)}, bf16[1,128,512]{2,1,0:T(8,128)(2,1)S(1)}, u32[]{:S(2)}, u32[]{:S(2)}) collective-permute-start(bf16[1,128,512]{2,1,0:T(8,128)(2,1)S(1)} %shard_map.70.refs_0_), channel_id=1, source_target_pairs={{0,1},{1,0},{2,3},{3,2},{4,5},{5,4},{6,7},{7,6},{8,9},{9,8},{10,11... | collective-permute-start | bytes 393224 | tf_op jit(solution)/shard_map/ppermute | solution.py:31
  240.4 25.3 %all-to-all-start.5 = ((bf16[4,3,128,512]{3,2,1,0:T(8,128)(2,1)}), bf16[4,3,128,512]{3,2,1,0:T(8,128)(2,1)S(1)}, u32[]{:S(2)}, u32[]{:S(2)}) async-start(bf16[4,3,128,512]{3,2,1,0:T(8,128)(2,1)} %copy-done.1), calls=%async_computation.5 | async-start | bytes 3145728 | tf_op jit(solution)/shard_map/all_to_all | solution.py:26
  246.1 15.6 %collective-permute-start.23 = (bf16[1,128,512]{2,1,0:T(8,128)(2,1)S(1)}, bf16[1,128,512]{2,1,0:T(8,128)(2,1)S(1)}, u32[]{:S(2)}, u32[]{:S(2)}) collective-permute-start(bf16[1,128,512]{2,1,0:T(8,128)(2,1)S(1)} %shard_map.67.refs_0_), channel_id=1, source_target_pairs={{0,1},{1,0},{2,3},{3,2},{4,5},{5,4},{6,7},{7,6},{8,9},{9,8},{10,11... | collective-permute-start | bytes 393224 | tf_op jit(solution)/shard_map/ppermute | solution.py:31
  265.7 12.9 %all-to-all-start.2 = ((bf16[4,1,128,512]{3,2,1,0:T(8,128)(2,1)}), bf16[4,1,128,512]{3,2,1,0:T(8,128)(2,1)}, u32[]{:S(2)}, u32[]{:S(2)}) async-start(bf16[4,1,128,512]{3,2,1,0:T(8,128)(2,1)} %copy-done.2), calls=%async_computation.2 | async-start | bytes 1048576 | tf_op jit(solution)/shard_map/all_to_all | solution.py:26
  (11 other events, 17.2 us)
